TPU v7x, 128 devices: a whole 4x4x4 slice. The times are simulated.
128 devices in a mesh: grp: 8 (over y, core), dev: 16 (over x, z).
Axes of the slice: x: 4, y: 4, z: 4, core: 2. Of those that a mesh axis runs over, the one named last changes fastest.
Arguments:
- suffix_queries: bfloat16 [16384, 2048], P(('grp', 'dev')), may hold values from -12 to 12
- suffix_keys: bfloat16 [16384, 2048], P(('grp', 'dev')), may hold values from -12 to 12
- suffix_values: bfloat16 [16384, 2048], P(('grp', 'dev')), may hold values from -6 to 6
- layer_input: bfloat16 [16384, 2048], P(('grp', 'dev')), may hold values from -6 to 6
- suffix_lengths: int32 [128, 8], P(('grp', 'dev')), may hold values from 1 to 32, as said below
- request_group: int32 [128, 8], P(('grp', 'dev')), may hold values from 0 to 7, as said below
- prefix_keys: bfloat16 [8, 4096, 2048], P('grp', None, 'dev'), may hold values from -12 to 12
- prefix_values: bfloat16 [8, 4096, 2048], P('grp', None, 'dev'), may hold values from -6 to 6
- up_weight: bfloat16 [2048, 8192], P(None, ('grp', 'dev')), may hold values from -0.125 to 0.125
- up_bias: bfloat16 [8192], P(('grp', 'dev')), may hold values from -3 to 3
- down_weight: bfloat16 [8192, 2048], P(('grp', 'dev')), may hold values from -0.0625 to 0.0625
- down_bias: float32 [2048], replicated, may hold values from -3 to 3
- attn_gain: float32 [2048], replicated, may hold values from 0.5 to 1.5
- attn_shift: float32 [2048], replicated, may hold values from -2 to 2
- out_gain: float32 [2048], replicated, may hold values from 0.5 to 1.5
- out_shift: float32 [2048], replicated, may hold values from -2 to 2
Outputs:
- layer_output: bfloat16 [16384, 2048], P(('grp', 'dev'))
Inputs may be any that keep to these rules, and one draw needn't show every extreme that they name: `suffix_lengths`: each row lists one device's 8 requests in slot order; they fill its 128 slots exactly, and at least one of them has 32 tokens. `request_group`: the 8 requests of one row name every prefix exactly once.
All inputs are finite; a program needn't handle non-finite values.
Results may differ from a plain program's by a relative error of at most 0.014.
Values may be sent and summed in bfloat16 or wider, within the bound.
A program may use at most 128 MiB of HBM per device.

v0:
```python
import math

import jax
import jax.numpy as jnp
from jax import lax
from jax.sharding import PartitionSpec as P

HD = 128


norm_eps = 1e-12


def layer_norm(summed, norm_gain, norm_shift):
    row_mean = jnp.mean(summed, axis=-1, keepdims=True)
    centred = summed - row_mean
    spread = jnp.mean(centred * centred, axis=-1, keepdims=True)
    return centred * lax.rsqrt(spread + norm_eps) * norm_gain + norm_shift


def request_layout(lengths, slot_count):
    end_points = jnp.cumsum(lengths)
    starts = end_points - lengths
    positions = lax.iota(jnp.int32, slot_count)
    member = (positions[:, None] >= starts[None, :]) & (positions[:, None] < end_points[None, :])
    slot_ids = lax.iota(jnp.int32, lengths.shape[0])
    segment = jnp.sum(jnp.where(member, slot_ids[None, :], 0), axis=1)
    return (starts, segment)


def expand_rows(piece_rows, up_matrix, up_offset):
    product = jnp.dot(piece_rows, up_matrix, preferred_element_type=jnp.float32)
    return jax.nn.gelu(product + up_offset.astype(jnp.float32), approximate=True).astype(
        jnp.bfloat16
    )


def attend_prefix(arrived, cache_keys, cache_values):
    sources, row_count, part_width = arrived.shape
    local_heads = part_width // HD
    per_block = math.gcd(sources, max(1, 512 // row_count))
    query_blocks = arrived.reshape(sources // per_block, per_block * row_count, local_heads, HD)
    key_heads = cache_keys.reshape(-1, local_heads, HD)
    value_heads = cache_values.reshape(-1, local_heads, HD)

    def one_block(query_block):
        scores = jnp.einsum(
            "qhd,khd->hqk", query_block, key_heads, preferred_element_type=jnp.float32
        ) * HD ** (-0.5)
        row_top = jnp.max(scores, axis=2).astype(jnp.bfloat16)
        weights = jnp.exp(
            scores - lax.optimization_barrier(row_top).astype(jnp.float32)[:, :, None]
        )
        row_sum = jnp.sum(weights, axis=2)
        mixed_sum = jnp.einsum(
            "hqk,khd->qhd",
            weights.astype(jnp.bfloat16),
            value_heads,
            preferred_element_type=jnp.float32,
        )
        answer = (mixed_sum / row_sum.T[:, :, None]).astype(jnp.bfloat16)
        return (answer.reshape(-1, part_width), row_top.T, row_sum.T.astype(jnp.bfloat16))

    answer, row_top, row_sum = lax.map(one_block, query_blocks)
    return (
        answer.reshape(sources, row_count, part_width),
        row_top.reshape(sources, row_count, local_heads),
        row_sum.reshape(sources, row_count, local_heads),
    )


def attend_suffix(query_rows, key_rows, value_rows, segment, head_count):
    slot_count = query_rows.shape[0]
    query_heads = query_rows.reshape(slot_count, head_count, HD)
    key_heads = key_rows.reshape(slot_count, head_count, HD)
    value_heads = value_rows.reshape(slot_count, head_count, HD)
    scores = jnp.einsum(
        "qhd,khd->hqk", query_heads, key_heads, preferred_element_type=jnp.float32
    ) * HD ** (-0.5)
    positions = lax.iota(jnp.int32, slot_count)
    visible = ((segment[:, None] == segment[None, :]) & (positions[None, :] <= positions[:, None]))[
        None
    ]
    row_top = jnp.max(jnp.where(visible, scores, -jnp.inf), axis=2)
    weights = jnp.where(visible, jnp.exp(scores - row_top[:, :, None]), 0.0)
    row_sum = jnp.sum(weights, axis=2)
    mixed_sum = jnp.einsum(
        "hqk,khd->qhd",
        weights.astype(jnp.bfloat16),
        value_heads,
        preferred_element_type=jnp.float32,
    )
    return (row_top.T, row_sum.T, mixed_sum)


def merge_parts(far_answer, far_top, far_sum, own_top, own_sum, own_mixed):
    far_top = far_top.astype(jnp.float32)
    far_sum = far_sum.astype(jnp.float32)
    joint_top = jnp.maximum(far_top, own_top)
    far_weight = jnp.exp(far_top - joint_top) * far_sum
    own_weight = jnp.exp(own_top - joint_top)
    numerator = (
        far_weight[:, :, None] * far_answer.astype(jnp.float32) + own_weight[:, :, None] * own_mixed
    )
    return numerator / (far_weight + own_weight * own_sum)[:, :, None]


def on_device(
    suffix_queries,
    suffix_keys,
    suffix_values,
    layer_input,
    suffix_lengths,
    request_group,
    prefix_keys,
    prefix_values,
    up_weight,
    up_bias,
    down_weight,
    down_bias,
    attn_gain,
    attn_shift,
    out_gain,
    out_shift,
):
    slot_count, model_width = suffix_queries.shape
    head_count = model_width // HD
    group_count = lax.axis_size("grp")
    column_count = lax.axis_size("dev")
    part_width = model_width // column_count
    local_heads = part_width // HD
    capacity = 2 * slot_count // group_count
    lengths = suffix_lengths[0]
    groups = request_group[0]
    request_total = lengths.shape[0]
    starts, segment = request_layout(lengths, slot_count)
    anchor = jnp.zeros((), jnp.int32)
    padded = jnp.concatenate(
        [suffix_queries, jnp.zeros((capacity, model_width), jnp.bfloat16)], axis=0
    )
    slot_rank = lax.iota(jnp.int32, capacity)
    outgoing = jnp.zeros((group_count, column_count, capacity, part_width), jnp.bfloat16)
    for request in range(request_total):
        taken = lax.dynamic_slice_in_dim(padded, starts[request], capacity, 0)
        taken = jnp.where((slot_rank < lengths[request])[:, None], taken, jnp.zeros_like(taken))
        split_rows = taken.reshape(capacity, column_count, part_width).transpose(1, 0, 2)
        outgoing = lax.dynamic_update_slice(
            outgoing, split_rows[None], (groups[request], anchor, anchor, anchor)
        )
    cache_keys = prefix_keys[0]
    cache_values = prefix_values[0]
    answer_part, top_part, sum_part = attend_prefix(
        lax.all_to_all(
            outgoing.reshape(group_count * column_count, capacity, part_width),
            ("grp", "dev"),
            split_axis=0,
            concat_axis=0,
            tiled=True,
        ),
        cache_keys,
        cache_values,
    )
    answer = lax.all_to_all(answer_part, ("grp", "dev"), split_axis=0, concat_axis=0, tiled=True)
    far_top = lax.all_to_all(top_part, ("grp", "dev"), split_axis=0, concat_axis=0, tiled=True)
    far_sum = lax.all_to_all(sum_part, ("grp", "dev"), split_axis=0, concat_axis=0, tiled=True)
    answer = answer.reshape(group_count, column_count, capacity, part_width)
    far_top = far_top.reshape(group_count, column_count, capacity, local_heads)
    far_sum = far_sum.reshape(group_count, column_count, capacity, local_heads)
    placed_answer = jnp.zeros((slot_count + capacity, model_width), jnp.bfloat16)
    placed_top = jnp.zeros((slot_count + capacity, head_count), jnp.bfloat16)
    placed_sum = jnp.zeros((slot_count + capacity, head_count), jnp.bfloat16)
    for request in range(request_total):
        own_answer = (
            lax.dynamic_index_in_dim(answer, groups[request], 0, keepdims=False)
            .transpose(1, 0, 2)
            .reshape(capacity, model_width)
        )
        own_top_rows = (
            lax.dynamic_index_in_dim(far_top, groups[request], 0, keepdims=False)
            .transpose(1, 0, 2)
            .reshape(capacity, head_count)
        )
        own_sum_rows = (
            lax.dynamic_index_in_dim(far_sum, groups[request], 0, keepdims=False)
            .transpose(1, 0, 2)
            .reshape(capacity, head_count)
        )
        placed_answer = lax.dynamic_update_slice(
            placed_answer, own_answer, (starts[request], anchor)
        )
        placed_top = lax.dynamic_update_slice(placed_top, own_top_rows, (starts[request], anchor))
        placed_sum = lax.dynamic_update_slice(placed_sum, own_sum_rows, (starts[request], anchor))
    own_top, own_sum, own_mixed = attend_suffix(
        suffix_queries, suffix_keys, suffix_values, segment, head_count
    )
    far_rows = placed_answer[:slot_count].reshape(slot_count, head_count, HD)
    context = merge_parts(
        far_rows, placed_top[:slot_count], placed_sum[:slot_count], own_top, own_sum, own_mixed
    )
    hidden_state = layer_norm(
        layer_input.astype(jnp.float32) + context.reshape(slot_count, model_width),
        attn_gain,
        attn_shift,
    ).astype(jnp.bfloat16)
    up_slice, bias_slice, down_slice = (
        lax.all_gather(up_weight, "grp", axis=1, tiled=True),
        lax.all_gather(up_bias, "grp", axis=0, tiled=True),
        lax.all_gather(down_weight, "grp", axis=0, tiled=True),
    )
    activation = expand_rows(
        lax.all_gather(hidden_state, "dev", axis=0, tiled=True), up_slice, bias_slice
    )
    mlp_sum = lax.psum_scatter(
        jnp.dot(activation, down_slice, preferred_element_type=jnp.float32).astype(jnp.bfloat16),
        "dev",
        scatter_dimension=0,
        tiled=True,
    ).astype(jnp.float32)
    return layer_norm(
        hidden_state.astype(jnp.float32) + mlp_sum + down_bias, out_gain, out_shift
    ).astype(jnp.bfloat16)


def solution(mesh):
    placed = (
        P(("grp", "dev"), None),
        P(("grp", "dev"), None),
        P(("grp", "dev"), None),
        P(("grp", "dev"), None),
        P(("grp", "dev"), None),
        P(("grp", "dev"), None),
        P("grp", None, "dev"),
        P("grp", None, "dev"),
        P(None, ("grp", "dev")),
        P(("grp", "dev")),
        P(("grp", "dev"), None),
        P(),
        P(),
        P(),
        P(),
        P(),
    )
    return jax.shard_map(
        on_device, mesh=mesh, in_specs=placed, out_specs=P(("grp", "dev"), None), check_vma=False
    )
```

profile of v0, /device:TPU:1, one launch (start us, length us, event | category | flops | bytes accessed | tf_op | source)
XLA Modules:
  0.0 411.9 jit_solution(14731411691771604662)
XLA Ops:
  7.3 0.8 reduce-window.4
  19.4 1.6 fusion.105
  31.0 1.6 fusion.103
  47.8 1.1 fusion.62
  48.9 1.2 broadcast_in_dim.147
  50.7 1.7 fusion.64
  57.2 11.6 %all-to-all-start = ((bf16[128,32,128]{2,1,0:T(8,128)(2,1)}), bf16[128,32,128]{2,1,0:T(8,128)(2,1)S(1)}, u32[]{:S(2)}, u32[]{:S(2)}) async-start(bf16[128,32,128]{2,1,0:T(8,128)(2,1)} %bitcast.51), calls=%async_computation | async-start | bytes 2097152 | tf_op jit(solution)/shard_map/all_to_all | solution.py:153
  69.6 17.8 %all-to-all-done = bf16[128,32,128]{2,1,0:T(8,128)(2,1)S(1)} async-done(((bf16[128,32,128]{2,1,0:T(8,128)(2,1)}), bf16[128,32,128]{2,1,0:T(8,128)(2,1)S(1)}, u32[]{:S(2)}, u32[]{:S(2)}) %all-to-all-start) | async-done | bytes 1048608 | tf_op jit(solution)/shard_map/all_to_all | solution.py:153
  87.4 41.1 %while.14 = (s32[]{:T(128)}, bf16[8,512,128]{2,1,0:T(8,128)(2,1)}, bf16[8,512,1]{1,0,2:T(8,128)(2,1)S(1)}, bf16[8,512,1]{1,0,2:T(8,128)(2,1)S(1)}, bf16[8,512,1,...) while((s32[]{:T(128)}, bf16[8,512,128]{2,1,0:T(8,128)(2,1)}, ...), condition=%wide.region_4.5_spmd, body=%wide.region_1.4_spmd.sunk | while | flops 1090650112 | bytes 31745168 | solution.py:64
  87.4 1.3 multiply_reduce_fusion.4
  88.8 1.5 fusion.118
  90.3 2.1 fusion.119
  92.6 1.3 multiply_reduce_fusion.4
  93.9 1.5 fusion.118
  95.4 2.2 fusion.119
  97.7 1.3 multiply_reduce_fusion.4
  99.1 1.5 fusion.118
  100.6 2.1 fusion.119
  102.8 1.3 multiply_reduce_fusion.4
  104.2 1.5 fusion.118
  105.7 2.1 fusion.119
  108.0 1.3 multiply_reduce_fusion.4
  109.3 1.5 fusion.118
  110.9 2.1 fusion.119
  113.1 1.3 multiply_reduce_fusion.4
  114.5 1.5 fusion.118
  116.0 2.1 fusion.119
  118.2 1.3 multiply_reduce_fusion.4
  119.6 1.5 fusion.118
  121.1 2.1 fusion.119
  123.4 1.3 multiply_reduce_fusion.4
  124.7 1.5 fusion.118
  126.3 2.2 fusion.119
  129.2 4.8 %all-to-all-start.2 = ((bf16[128,32,1]{1,2,0:T(2,128)(2,1)}), bf16[128,32,1]{1,2,0:T(2,128)(2,1)S(1)}, u32[]{:S(2)}, u32[]{:S(2)}) async-start(bf16[128,32,1]{1,2,0:T(2,128)(2,1)} %reshape.401), calls=%async_computation.2 | async-start | bytes 131072 | tf_op jit(solution)/shard_map/all_to_all | solution.py:165
  134.8 8.9 %all-to-all-done.2 = bf16[128,32,1]{1,2,0:T(2,128)(2,1)S(1)} async-done(((bf16[128,32,1]{1,2,0:T(2,128)(2,1)}), bf16[128,32,1]{1,2,0:T(2,128)(2,1)S(1)}, u32[]{:S(2)}, u32[]{:S(2)}) %all-to-all-start.2) | async-done | bytes 8224 | tf_op jit(solution)/shard_map/all_to_all | solution.py:165
  143.7 4.5 %all-to-all-start.1 = ((bf16[128,32,1]{1,2,0:T(2,128)(2,1)}), bf16[128,32,1]{1,2,0:T(2,128)(2,1)S(1)}, u32[]{:S(2)}, u32[]{:S(2)}) async-start(bf16[128,32,1]{1,2,0:T(2,128)(2,1)} %reshape.400), calls=%async_computation.1 | async-start | bytes 131072 | tf_op jit(solution)/shard_map/all_to_all | solution.py:164
  148.3 9.4 %all-to-all-done.1 = bf16[128,32,1]{1,2,0:T(2,128)(2,1)S(1)} async-done(((bf16[128,32,1]{1,2,0:T(2,128)(2,1)}), bf16[128,32,1]{1,2,0:T(2,128)(2,1)S(1)}, u32[]{:S(2)}, u32[]{:S(2)}) %all-to-all-start.1) | async-done | bytes 8224 | tf_op jit(solution)/shard_map/all_to_all | solution.py:164
  157.8 4.5 %all-to-all-start.3 = ((bf16[128,32,128]{2,1,0:T(8,128)(2,1)}), bf16[128,32,128]{2,1,0:T(8,128)(2,1)S(1)}, u32[]{:S(2)}, u32[]{:S(2)}) async-start(bf16[128,32,128]{2,1,0:T(8,128)(2,1)} %bitcast.380), calls=%async_computation.3 | async-start | bytes 2097152 | tf_op jit(solution)/shard_map/all_to_all | solution.py:163
  162.4 2.0 copy.149
  165.1 1.0 copy-done.5
  170.6 10.4 %all-to-all-done.3 = bf16[128,32,128]{2,1,0:T(8,128)(2,1)S(1)} async-done(((bf16[128,32,128]{2,1,0:T(8,128)(2,1)}), bf16[128,32,128]{2,1,0:T(8,128)(2,1)S(1)}, u32[]{:S(2)}, u32[]{:S(2)}) %all-to-all-start.3) | async-done | bytes 1048608 | tf_op jit(solution)/shard_map/all_to_all | solution.py:163
  182.0 1.1 copy.141
  183.0 1.0 copy.140
  184.0 1.0 copy.139
  185.1 1.0 copy.138
  186.1 1.0 copy.137
  187.2 4.9 %dynamic_update_slice.131 = bf16[160,2048]{0,1:T(8,128)(2,1)S(1)} dynamic-update-slice(bf16[160,2048]{0,1:T(8,128)(2,1)S(1)} %broadcast_in_dim.168, bf16[32,2048]{0,1:T(8,128)(2,1)} %bitcast.379, s32[]{:T(128)S(6)} %select_n.134, s32[]{:T(128)} %constant.96.clone.1) | dynamic-update-slice | bytes 262148 | tf_op jit(solution)/shard_map/dynamic_update_slice | solution.py:188
  192.1 5.9 %dynamic_update_slice.132 = bf16[160,2048]{0,1:T(8,128)(2,1)S(1)} dynamic-update-slice(bf16[160,2048]{0,1:T(8,128)(2,1)S(1)} %dynamic_update_slice.131, bf16[32,2048]{0,1:T(8,128)(2,1)} %bitcast.378, s32[]{:T(128)S(6)} %select_n.137, s32[]{:T(128)} %constant.96.clone.1) | dynamic-update-slice | bytes 262148 | tf_op jit(solution)/shard_map/dynamic_update_slice | solution.py:188
  198.0 5.9 %dynamic_update_slice.133 = bf16[160,2048]{0,1:T(8,128)(2,1)S(1)} dynamic-update-slice(bf16[160,2048]{0,1:T(8,128)(2,1)S(1)} %dynamic_update_slice.132, bf16[32,2048]{0,1:T(8,128)(2,1)} %bitcast.377, s32[]{:T(128)S(6)} %select_n.140, s32[]{:T(128)} %constant.96.clone.1) | dynamic-update-slice | bytes 262148 | tf_op jit(solution)/shard_map/dynamic_update_slice | solution.py:188
  204.0 5.9 %dynamic_update_slice.134 = bf16[160,2048]{0,1:T(8,128)(2,1)S(1)} dynamic-update-slice(bf16[160,2048]{0,1:T(8,128)(2,1)S(1)} %dynamic_update_slice.133, bf16[32,2048]{0,1:T(8,128)(2,1)} %bitcast.376, s32[]{:T(128)S(6)} %select_n.143, s32[]{:T(128)} %constant.96.clone.1) | dynamic-update-slice | bytes 262148 | tf_op jit(solution)/shard_map/dynamic_update_slice | solution.py:188
  210.0 5.9 %dynamic_update_slice.135 = bf16[160,2048]{0,1:T(8,128)(2,1)S(1)} dynamic-update-slice(bf16[160,2048]{0,1:T(8,128)(2,1)S(1)} %dynamic_update_slice.134, bf16[32,2048]{0,1:T(8,128)(2,1)} %bitcast.375, s32[]{:T(128)S(6)} %select_n.146, s32[]{:T(128)} %constant.96.clone.1) | dynamic-update-slice | bytes 262148 | tf_op jit(solution)/shard_map/dynamic_update_slice | solution.py:188
  215.9 4.0 dynamic_update_slice.136
  219.9 4.0 dynamic_update_slice.137
  223.9 4.2 %dynamic_update_slice.138 = bf16[160,2048]{0,1:T(8,128)(2,1)S(1)} dynamic-update-slice(bf16[160,2048]{0,1:T(8,128)(2,1)S(1)} %dynamic_update_slice.137, bf16[32,2048]{0,1:T(8,128)(2,1)S(1)} %bitcast.372, s32[]{:T(128)S(6)} %select_n.155, s32[]{:T(128)} %constant.96.clone.1) | dynamic-update-slice | bytes 262148 | tf_op jit(solution)/shard_map/dynamic_update_slice | solution.py:188
  228.3 2.8 fusion.36
  231.1 1.6 copy.147
  233.2 1.1 add_convert_fusion.1
  235.9 13.3 %all-reduce.1 = bf16[512]{0:T(512)(128)(2,1)S(1)} all-reduce(bf16[512]{0:T(512)(128)(2,1)S(1)} %dynamic-update-slice), channel_id=1, replica_groups=mesh['grp'=8,'dev'=16] {'grp'}, use_global_device_ids=true, to_apply=%add.1 | all-reduce | flops 512 | bytes 2048
  249.2 52.4 %all-gather.4.cloned.1.call-done = bf16[2048,2048]{1,0:T(8,128)(2,1)} async-done(((bf16[128,2048]{1,0:T(8,128)(2,1)}), bf16[2048,2048]{1,0:T(8,128)(2,1)}) %all-gather.4.cloned.1.call-update) | async-done | bytes 8388624 | tf_op jit(solution)/shard_map/all_gather | solution.py:211
  301.6 15.2 %convolution_convert_fusion = bf16[2048,2048]{1,0:T(8,128)(2,1)} fusion(bf16[512,2048]{1,0:T(8,128)(2,1)} %all-gather.8.cloned.1.call-done, bf16[2048,2048]{1,0:T(8,128)(2,1)} %all-gather.4.cloned.1.call-done, bf16[2048,512]{0,1:T(8,128)(2,1)} %all-gather.6.cloned.1.call-done, f32[512]{0:T(512)S(1)} %convert_element_type.97), kind=kOutput, calls=%fused_computation.17 | convolution fusion | flops 8604614656 | bytes 20973568 | tf_op jit(solution)/shard_map/dot_general | solution.py:214
  316.8 83.7 %reduce-scatter.2.cloned.1.call-done = bf16[128,2048]{1,0:T(8,128)(2,1)} async-done(((bf16[2048,2048]{1,0:T(8,128)(2,1)}), bf16[128,2048]{1,0:T(8,128)(2,1)}) %reduce-scatter.2.cloned.1.call-update) | async-done | bytes 524304 | tf_op jit(solution)/shard_map/reduce_scatter | solution.py:213
  400.5 1.3 fusion.39
  401.8 1.4 multiply_reduce_fusion.1
  403.2 2.2 add_convert_fusion
  (175 shorter events, 23.5 us)
Async XLA Ops:
  6.5 158.0 %copy-start = (bf16[128,2048]{1,0:T(8,128)(2,1)S(1)}, bf16[128,2048]{1,0:T(8,128)(2,1)}, u32[]{:S(2)}) copy-start(bf16[128,2048]{1,0:T(8,128)(2,1)} %param.19) | copy-start | bytes 1572868
  6.5 80.9 %copy-start.1 = (bf16[1,4096,128]{2,1,0:T(8,128)(2,1)S(1)}, bf16[1,4096,128]{2,1,0:T(8,128)(2,1)}, u32[]{:S(2)}) copy-start(bf16[1,4096,128]{2,1,0:T(8,128)(2,1)} %param.24) | copy-start | bytes 3145732
  6.5 242.6 %all-gather.6.cloned.1.call-start = ((), (), s32[]{:S(2)}) async-start(), calls=%async_computation.6 | async-start | bytes 2359296 | tf_op jit(solution)/shard_map/all_gather | solution.py:206
  57.2 30.2 %all-to-all-start = ((bf16[128,32,128]{2,1,0:T(8,128)(2,1)}), bf16[128,32,128]{2,1,0:T(8,128)(2,1)S(1)}, u32[]{:S(2)}, u32[]{:S(2)}) async-start(bf16[128,32,128]{2,1,0:T(8,128)(2,1)} %bitcast.51), calls=%async_computation | async-start | bytes 2097152 | tf_op jit(solution)/shard_map/all_to_all | solution.py:153
  68.8 180.4 %all-gather.8.cloned.1.call-start = ((), (), s32[]{:S(2)}) async-start(), calls=%async_computation.7 | async-start | bytes 2359296 | tf_op jit(solution)/shard_map/all_gather | solution.py:208
  87.4 60.9 %copy-start.7 = (s32[1,8]{1,0:T(1,128)S(1)}, s32[1,8]{1,0:T(1,128)}, u32[]{:S(2)}) copy-start(s32[1,8]{1,0:T(1,128)} %param.22) | copy-start | bytes 100
  87.4 77.2 %copy-start.4 = (bf16[128,2048]{1,0:T(8,128)(2,1)S(1)}, bf16[128,2048]{1,0:T(8,128)(2,1)}, u32[]{:S(2)}) copy-start(bf16[128,2048]{1,0:T(8,128)(2,1)} %param.18) | copy-start | bytes 1572868
  88.8 1.5 copy-start.12
  93.9 1.5 copy-start.12
  99.1 1.5 copy-start.12
  104.2 1.5 copy-start.12
  109.3 1.5 copy-start.12
  114.5 1.5 copy-start.12
  119.6 1.5 copy-start.12
  124.7 1.5 copy-start.12
  129.2 14.5 %all-to-all-start.2 = ((bf16[128,32,1]{1,2,0:T(2,128)(2,1)}), bf16[128,32,1]{1,2,0:T(2,128)(2,1)S(1)}, u32[]{:S(2)}, u32[]{:S(2)}) async-start(bf16[128,32,1]{1,2,0:T(2,128)(2,1)} %reshape.401), calls=%async_computation.2 | async-start | bytes 131072 | tf_op jit(solution)/shard_map/all_to_all | solution.py:165
  143.7 14.0 %all-to-all-start.1 = ((bf16[128,32,1]{1,2,0:T(2,128)(2,1)}), bf16[128,32,1]{1,2,0:T(2,128)(2,1)S(1)}, u32[]{:S(2)}, u32[]{:S(2)}) async-start(bf16[128,32,1]{1,2,0:T(2,128)(2,1)} %reshape.400), calls=%async_computation.1 | async-start | bytes 131072 | tf_op jit(solution)/shard_map/all_to_all | solution.py:164
  157.8 23.2 %all-to-all-start.3 = ((bf16[128,32,128]{2,1,0:T(8,128)(2,1)}), bf16[128,32,128]{2,1,0:T(8,128)(2,1)S(1)}, u32[]{:S(2)}, u32[]{:S(2)}) async-start(bf16[128,32,128]{2,1,0:T(8,128)(2,1)} %bitcast.380), calls=%async_computation.3 | async-start | bytes 2097152 | tf_op jit(solution)/shard_map/all_to_all | solution.py:163
  162.3 139.2 %all-gather.4.cloned.1.call-start = ((), (), s32[]{:S(2)}) async-start(), calls=%async_computation.5 | async-start | bytes 8912896 | tf_op jit(solution)/shard_map/all_gather | solution.py:211
  165.1 1.0 copy-start.5
  228.2 4.4 %copy-start.3 = (bf16[128,2048]{1,0:T(8,128)(2,1)S(1)}, bf16[128,2048]{1,0:T(8,128)(2,1)}, u32[]{:S(2)}) copy-start(bf16[128,2048]{1,0:T(8,128)(2,1)} %param.21) | copy-start | bytes 1572868
  228.2 4.9 %copy-start.8 = (f32[2048]{0:T(1024)S(1)}, f32[2048]{0:T(1024)}, u32[]{:S(2)}) copy-start(f32[2048]{0:T(1024)} %param.31) | copy-start | bytes 24580
  228.2 4.9 %copy-start.9 = (f32[2048]{0:T(1024)S(1)}, f32[2048]{0:T(1024)}, u32[]{:S(2)}) copy-start(f32[2048]{0:T(1024)} %param.30) | copy-start | bytes 24580
  231.1 3.3 copy-start.14
  231.1 4.5 %copy-start.13 = (bf16[64]{0:T(256)(128)(2,1)S(1)}, bf16[64]{0:T(256)(128)(2,1)}, u32[]{:S(2)}) copy-start(bf16[64]{0:T(256)(128)(2,1)} %param.27) | copy-start | bytes 388
  234.3 166.2 %reduce-scatter.2.cloned.1.call-start = ((), (), s32[]{:S(2)}) async-start(), calls=%async_computation.8 | async-start | bytes 8912896 | tf_op jit(solution)/shard_map/reduce_scatter | solution.py:213
  316.8 83.7 %copy-start.2 = (bf16[128,2048]{1,0:T(8,128)(2,1)S(1)}, bf16[128,2048]{1,0:T(8,128)(2,1)}, u32[]{:S(2)}) copy-start(bf16[128,2048]{1,0:T(8,128)(2,1)} %add_convert_fusion.1) | copy-start | bytes 1572868
  316.8 83.7 %copy-start.6 = (f32[2048]{0:T(1024)S(1)}, f32[2048]{0:T(1024)}, u32[]{:S(2)}) copy-start(f32[2048]{0:T(1024)} %param.29) | copy-start | bytes 24580
  316.8 86.4 %copy-start.10 = (f32[2048]{0:T(1024)S(1)}, f32[2048]{0:T(1024)}, u32[]{:S(2)}) copy-start(f32[2048]{0:T(1024)} %param.33) | copy-start | bytes 24580
  316.8 86.4 %copy-start.11 = (f32[2048]{0:T(1024)S(1)}, f32[2048]{0:T(1024)}, u32[]{:S(2)}) copy-start(f32[2048]{0:T(1024)} %param.32) | copy-start | bytes 24580
Sparse Core Ops, SparseCore 0:
  9.1 28.7 all-gather.5
  71.3 27.0 all-gather.7
  234.4 67.1 all-gather.3
  316.9 83.5 reduce-scatter.1
where the time goes:
time: 414 us; the launch traced here: 412 us
  waiting for transfers between devices  184 us (44%)
  local copies, waits for them, and re-layouts  69.7 us (17%)
  matrix products  46.3 us (11%)
  between operations  44.2 us (11%)
  other arithmetic  28.4 us (7%)
  starting transfers between devices  25.6 us (6%)
  blocking collectives  13.3 us (3%)
    reduce_scatter x1, waiting for transfers between devices, on_device(): lax.psum_scatter(jnp.dot(activation, down_slice, preferred_element_type=j...  83.7 us
    all_gather x1, waiting for transfers between devices, on_device(): lax.all_gather(hidden_state, 'dev', axis=0, tiled=True)  52.4 us
    dynamic_update_slice x8, local copies, waits for them, and re-layouts, on_device(): lax.dynamic_update_slice(placed_answer, own_answer, (starts[request], anc...  40.9 us
    all_to_all x1, waiting for transfers between devices, on_device(): lax.all_to_all(outgoing.reshape(group_count * column_count, capacity, par...  17.8 us
    dot_general x8, matrix products, one_block(): jnp.einsum('hqk,khd->qhd', weights.astype(jnp.bfloat16), value_heads, pre...  17.2 us
    dot_general x1, matrix products, on_device(): jnp.dot(activation, down_slice, preferred_element_type=jnp.float32)  15.2 us
    unnamed x1, blocking collectives  13.3 us
    reduce_sum x8, other arithmetic, one_block(): row_sum = jnp.sum(weights, axis=2)  12 us
  transfers between devices with their start and end apart: 8, of which 6 were waited for; matrix products, arithmetic and copies ran while one was open for 30% of the time, Pallas kernels for 0%

commit v1 on v0

v1 whole, which is shorter than its diff:
```python
import functools

import jax
import jax.numpy as jnp
from jax import lax
from jax.experimental import pallas as pl
from jax.experimental.pallas import tpu as pltpu
from jax.sharding import Mesh, PartitionSpec as P

HD = 128
NY, NC, NX, NZ = 4, 2, 4, 4
GRP, DEV = NY * NC, NX * NZ
CAP = 32
LOG2E = 1.4426950408889634
SCALE2 = HD**-0.5 * LOG2E
NORM_EPS = 1e-12
NEG = -1e30
MESH = pl.DeviceIdType.MESH
NT_DIMS = (((1,), (1,)), ((), ()))
LIMIT = 64 * 1024 * 1024 - 65536


def coordinates():
    return tuple(lax.axis_index(name) for name in ("y", "c", "x", "z"))


def place(y, c, x, z):
    return {"y": y, "c": c, "x": x, "z": z}


def plane_at(x, z, block):
    return lax.rem(x + block // NZ, NX), lax.rem(z + lax.rem(block, NZ), NZ)


def plane_back(x, z, block):
    return lax.rem(x + NX - block // NZ, NX), lax.rem(z + NZ - lax.rem(block, NZ), NZ)


def wait_bytes(ref, sem):
    pltpu.make_async_copy(ref, ref, sem).wait()


def norm_rows(summed, gain, shift):
    mean = jnp.mean(summed, axis=-1, keepdims=True)
    centred = summed - mean
    spread = jnp.mean(centred * centred, axis=-1, keepdims=True)
    return centred * lax.rsqrt(spread + NORM_EPS) * gain + shift


def slot_tables(len_ref, grp_ref, shape, dim):
    slot = lax.broadcasted_iota(jnp.int32, shape, dim)
    start = jnp.int32(0)
    group = jnp.zeros(shape, jnp.int32)
    rank = jnp.zeros(shape, jnp.int32)
    for request in range(len_ref.shape[1]):
        length = len_ref[0, request]
        inside = (slot >= start) & (slot < start + length)
        group = jnp.where(inside, grp_ref[0, request], group)
        rank = jnp.where(inside, slot - start, rank)
        start = start + length
    return group, rank


def prefix_kernel(
    len_ref, grp_ref, q_ref, k_ref, v_ref, x_ref, bias_ref, pk_ref, pv_ref, gain_ref, shift_ref,
    hid_ref, bias_out,
    qs, qr, ans_s, ans_r, lse_s, lse_r, bias_r, s0, s1, p0, p1, acc, lcol, lsecol, mixed, own_top, own_sum,
    q_send, q_recv, a_send, a_recv, l_send, l_recv, b_send, b_recv, self_sem,
):
    y, c, x, z = coordinates()
    me_g = y * NC + c
    me_d = x * NZ + z
    slots = q_ref.shape[0]
    heads = q_ref.shape[1] // HD
    s_bufs, p_bufs = (s0, s1), (p0, p1)
    rows = GRP * CAP
    plen = pk_ref.shape[0]

    def group_at(k):
        g = lax.rem(me_g + k, GRP)
        return g, g // NC, lax.rem(g, NC)

    barrier = pltpu.get_barrier_semaphore()

    def greet(block, k):
        tx, tz = plane_at(x, z, block)
        _, ty, tc = group_at(k)
        pl.semaphore_signal(barrier, inc=1, device_id=place(ty, tc, tx, tz), device_id_type=MESH)

    for k in range(1, GRP):
        greet(0, k)

    @pl.loop(1, DEV)
    def _(block):
        for k in range(GRP):
            greet(block, k)

    group_row, rank_row = slot_tables(len_ref, grp_ref, (1, slots), 1)
    pick = lax.broadcasted_iota(jnp.int32, (rows, slots), 0) == group_row * CAP + rank_row
    pick = pick.astype(jnp.float32).astype(jnp.bfloat16)
    for d in range(heads):
        packed = jnp.dot(pick, q_ref[:, d * HD : (d + 1) * HD], preferred_element_type=jnp.float32)
        packed = packed.astype(jnp.bfloat16).reshape(GRP, CAP, HD)
        for g in range(GRP):
            qs[g * DEV + d] = packed[g]
    pl.semaphore_wait(barrier, GRP * DEV - 1)

    def send_query(block, k):
        tx, tz = plane_at(x, z, block)
        g, ty, tc = group_at(k)
        pltpu.make_async_remote_copy(
            src_ref=qs.at[g * DEV + tx * NZ + tz],
            dst_ref=qr.at[block * GRP + me_g],
            send_sem=q_send,
            recv_sem=q_recv.at[block],
            device_id=place(ty, tc, tx, tz),
            device_id_type=MESH,
        ).start()

    own_query = pltpu.make_async_copy(qs.at[me_g * DEV + me_d], qr.at[me_g], self_sem.at[0])
    own_query.start()
    for k in range(1, GRP):
        send_query(0, k)

    @pl.loop(1, DEV)
    def _(block):
        for k in range(GRP):
            send_query(block, k)

    for k in range(1, NC * DEV):
        tc = lax.rem(c + k // DEV, NC)
        tx, tz = plane_at(x, z, k % DEV)
        pltpu.make_async_remote_copy(
            src_ref=bias_ref,
            dst_ref=bias_r.at[c * DEV + me_d],
            send_sem=b_send,
            recv_sem=b_recv,
            device_id=place(y, tc, tx, tz),
            device_id_type=MESH,
        ).start()
    own_bias = pltpu.make_async_copy(bias_ref, bias_r.at[c * DEV + me_d], self_sem.at[3])
    own_bias.start()

    group_col, rank_col = slot_tables(len_ref, grp_ref, (slots, 1), 0)
    visible = (group_col == group_row) & (
        lax.broadcasted_iota(jnp.int32, (slots, slots), 1)
        <= lax.broadcasted_iota(jnp.int32, (slots, slots), 0)
    )

    @pl.loop(0, heads)
    def _(h):
        cols = pl.ds(pl.multiple_of(h * HD, HD), HD)
        s = lax.dot_general(q_ref[:, cols], k_ref[:, cols], NT_DIMS, preferred_element_type=jnp.float32)
        s = jnp.where(visible, s * SCALE2, NEG)
        top = jnp.max(s, axis=1, keepdims=True)
        w = jnp.where(visible, jnp.exp2(s - top), 0.0)
        own_top[h] = top
        own_sum[h] = jnp.sum(w, axis=1, keepdims=True)
        mixed[:, cols] = jnp.dot(w.astype(jnp.bfloat16), v_ref[:, cols], preferred_element_type=jnp.float32)

    def answer_back(block, k):
        tx, tz = plane_back(x, z, block)
        g, ty, tc = group_at(k)
        where = place(ty, tc, tx, tz)
        pltpu.make_async_remote_copy(
            src_ref=ans_s.at[block * GRP + g],
            dst_ref=ans_r.at[me_d * GRP + me_g],
            send_sem=a_send, recv_sem=a_recv, device_id=where, device_id_type=MESH,
        ).start()
        pltpu.make_async_remote_copy(
            src_ref=lse_s.at[block * GRP + g],
            dst_ref=lse_r.at[me_d * GRP + me_g],
            send_sem=l_send, recv_sem=l_recv, device_id=where, device_id_type=MESH,
        ).start()

    steps = 8
    span = plen // steps
    part = rows // steps

    def stage(i, parity, scoring, weighing, mixing, first=False):
        other = 1 - parity
        if scoring:
            if first:
                wait_bytes(qr.at[pl.ds(0, GRP - 1)], q_recv.at[0])
                own_query.wait()
            else:
                wait_bytes(qr.at[pl.ds(i * GRP, GRP)], q_recv.at[i])
        if mixing:
            acc[...] = jnp.zeros_like(acc)

        @pl.loop(0, steps)
        def _(j):
            keys = pl.ds(pl.multiple_of(j * span, span), span)
            if scoring:
                block = qr[pl.ds(i * GRP, GRP)].reshape(rows, HD)
                s_bufs[parity][:, keys] = lax.dot_general(
                    block, pk_ref[keys, :], NT_DIMS, preferred_element_type=jnp.float32
                )
            if weighing:
                some = pl.ds(pl.multiple_of(j * part, part), part)
                s = s_bufs[other][some, :]
                top = jnp.max(s, axis=1, keepdims=True) * SCALE2
                w = jnp.exp2(s * SCALE2 - top)
                total = jnp.sum(w, axis=1, keepdims=True)
                p_bufs[other][some, :] = w.astype(jnp.bfloat16)
                lcol[other, some, :] = total
                lsecol[other, some, :] = top + jnp.log(total) * LOG2E
            if mixing:
                acc[...] += jnp.dot(p_bufs[parity][:, keys], pv_ref[keys, :], preferred_element_type=jnp.float32)

        if mixing:
            done = i - 2
            answer = (acc[...] / lcol[parity]).astype(jnp.bfloat16).reshape(GRP, CAP, HD)
            spread = jnp.broadcast_to(lsecol[parity], (rows, HD)).reshape(GRP, CAP, HD)
            diagonal = lax.broadcasted_iota(jnp.int32, (GRP, CAP, HD), 1) == lax.broadcasted_iota(
                jnp.int32, (GRP, CAP, HD), 2
            )
            lines = jnp.sum(jnp.where(diagonal, spread, 0.0), axis=1)
            for g in range(GRP):
                ans_s[done * GRP + g] = answer[g]
                lse_s[done * GRP + g] = lines[g : g + 1]

    def send_back(done):
        for k in range(GRP):
            answer_back(done, k)

    stage(0, 0, True, False, False, first=True)
    stage(1, 1, True, True, False)
    stage(2, 0, True, True, True)
    own_answer = pltpu.make_async_copy(ans_s.at[me_g], ans_r.at[me_d * GRP + me_g], self_sem.at[1])
    own_lse = pltpu.make_async_copy(lse_s.at[me_g], lse_r.at[me_d * GRP + me_g], self_sem.at[2])
    own_answer.start()
    own_lse.start()
    for k in range(1, GRP):
        answer_back(0, k)
    stage(3, 1, True, True, True)
    send_back(1)

    @pl.loop(2, DEV // 2)
    def _(pair):
        stage(2 * pair, 0, True, True, True)
        send_back(2 * pair - 2)
        stage(2 * pair + 1, 1, True, True, True)
        send_back(2 * pair - 1)

    stage(DEV, 0, False, True, True)
    send_back(DEV - 2)
    stage(DEV + 1, 1, False, False, True)
    send_back(DEV - 1)

    own_bias.wait()
    wait_bytes(bias_r.at[pl.ds(0, NC * DEV - 1)], b_recv)
    for half in range(NC):
        for e in range(DEV // 2):
            at = half * DEV + 2 * e
            bias_out[half : half + 1, e * HD : (e + 1) * HD] = bias_r[at] + bias_r[at + 1]

    own_answer.wait()
    own_lse.wait()
    wait_bytes(ans_r.at[pl.ds(0, GRP * DEV - 1)], a_recv)
    wait_bytes(lse_r.at[pl.ds(0, GRP * DEV - 1)], l_recv)
    unpick = lax.broadcasted_iota(jnp.int32, (slots, rows), 1) == group_col * CAP + rank_col
    unpick = unpick.astype(jnp.float32).astype(jnp.bfloat16)
    lane = lax.broadcasted_iota(jnp.int32, (slots, HD), 1)

    @pl.loop(0, heads)
    def _(h):
        cols = pl.ds(pl.multiple_of(h * HD, HD), HD)
        far = jnp.dot(
            unpick, ans_r[pl.ds(h * GRP, GRP)].reshape(rows, HD), preferred_element_type=jnp.float32
        )
        spread = jnp.zeros((slots, HD), jnp.float32)
        for g in range(GRP):
            spread = jnp.where(group_col == g, lse_r[h * GRP + g], spread)
        far_top = jnp.sum(jnp.where(lane == rank_col, spread, 0.0), axis=1, keepdims=True)
        top = own_top[h]
        joint = jnp.maximum(far_top, top)
        far_weight = jnp.exp2(far_top - joint)
        own_weight = jnp.exp2(top - joint)
        below = far_weight + own_weight * own_sum[h]
        mixed[:, cols] = (far_weight * far + own_weight * mixed[:, cols]) / below

    @pl.loop(0, slots // 16)
    def _(r):
        some = pl.ds(pl.multiple_of(r * 16, 16), 16)
        summed = x_ref[some, :].astype(jnp.float32) + mixed[some, :]
        hid_ref[some, :] = norm_rows(summed, gain_ref[...], shift_ref[...]).astype(jnp.bfloat16)

    wait_bytes(qs.at[pl.ds(0, GRP * DEV - 1)], q_send)
    wait_bytes(ans_s.at[pl.ds(0, GRP * DEV - 1)], a_send)
    wait_bytes(lse_s.at[pl.ds(0, GRP * DEV - 1)], l_send)
    wait_bytes(bias_r.at[pl.ds(0, NC * DEV - 1)], b_send)


def mlp_kernel(
    hid_ref, bias_ref, up_ref, down_ref, dbias_ref, gain_ref, shift_ref,
    out_ref,
    tok, wu, wd, hidden, acc, part_s, part_r,
    w_sem, w_send, w_recv, t_send, t_recv, p_send, p_recv,
):
    y, c, x, z = coordinates()
    slots, width = hid_ref.shape
    steps_y = (0, 1, 3, 2)
    back = {1: 2, 2: 1, 3: 3}

    def at_y(pos):
        return place(lax.rem(y + steps_y[pos], NY), c, x, z)

    partner = place(y, 1 - c, x, z)
    barrier = pltpu.get_barrier_semaphore()
    for pos in (1, 2, 3):
        pl.semaphore_signal(barrier, inc=1, device_id=at_y(pos), device_id_type=MESH)
    pl.semaphore_signal(barrier, inc=1, device_id=partner, device_id_type=MESH)
    own_up = pltpu.make_async_copy(up_ref, wu.at[0], w_sem.at[0])
    own_down = pltpu.make_async_copy(down_ref, wd.at[0], w_sem.at[1])
    own_up.start()
    own_down.start()
    tok[0:slots, :] = hid_ref[...]
    pl.semaphore_wait(barrier, NY)

    def remote(src, dst, send_sem, recv_sem, where):
        return pltpu.make_async_remote_copy(
            src_ref=src, dst_ref=dst, send_sem=send_sem, recv_sem=recv_sem,
            device_id=where, device_id_type=MESH,
        )

    token_copies = {
        pos: remote(
            hid_ref, tok.at[pl.ds(back[pos] * slots, slots)],
            t_send.at[pos - 1], t_recv.at[back[pos] - 1], at_y(pos),
        )
        for pos in (1, 2, 3)
    }
    for pos in (3, 1, 2):
        token_copies[pos].start()
    weight_copies = (
        remote(up_ref, wu.at[1], w_send.at[0], w_recv.at[0], partner),
        remote(down_ref, wd.at[1], w_send.at[1], w_recv.at[1], partner),
    )
    for copy in weight_copies:
        copy.start()

    tile = 256
    units = wu.shape[2]

    def half_mlp(first, count, slot):
        rows = pl.ds(first * slots, count * slots)
        which = c if slot == 0 else 1 - c

        @pl.loop(0, units // tile)
        def _(n):
            cols = pl.ds(pl.multiple_of(n * tile, tile), tile)
            u = jnp.dot(tok[rows, :], wu[slot, :, cols], preferred_element_type=jnp.float32)
            u = u + bias_ref[pl.ds(which, 1), cols]
            hidden[rows, cols] = jax.nn.gelu(u, approximate=True).astype(jnp.bfloat16)

        @pl.loop(0, width // tile)
        def _(n):
            cols = pl.ds(pl.multiple_of(n * tile, tile), tile)
            m = jnp.dot(hidden[rows, :], wd[slot, :, cols], preferred_element_type=jnp.float32)
            if slot == 0:
                acc[rows, cols] = m
            else:
                acc[rows, cols] += m

    def send_partial(pos):
        part_s[pos - 1] = acc[pl.ds(pos * slots, slots), :].astype(jnp.bfloat16)
        copy = remote(
            part_s.at[pos - 1], part_r.at[back[pos] - 1], p_send.at[pos - 1], p_recv.at[back[pos] - 1], at_y(pos)
        )
        copy.start()
        return copy

    own_up.wait()
    own_down.wait()
    half_mlp(0, 1, 0)
    wait_bytes(tok.at[pl.ds(slots, slots)], t_recv.at[0])
    wait_bytes(tok.at[pl.ds(2 * slots, slots)], t_recv.at[1])
    half_mlp(1, 2, 0)
    wait_bytes(wu.at[1], w_recv.at[0])
    wait_bytes(wd.at[1], w_recv.at[1])
    half_mlp(1, 2, 1)
    partials = [send_partial(1), send_partial(2)]
    wait_bytes(tok.at[pl.ds(3 * slots, slots)], t_recv.at[2])
    half_mlp(3, 1, 0)
    half_mlp(3, 1, 1)
    partials.append(send_partial(3))
    half_mlp(0, 1, 1)
    for pos in (1, 2, 3):
        wait_bytes(part_r.at[pos - 1], p_recv.at[pos - 1])

    @pl.loop(0, slots // 16)
    def _(r):
        some = pl.ds(pl.multiple_of(r * 16, 16), 16)
        total = acc[some, :] + hid_ref[some, :].astype(jnp.float32) + dbias_ref[...]
        for pos in range(3):
            total = total + part_r[pos, some, :].astype(jnp.float32)
        out_ref[some, :] = norm_rows(total, gain_ref[...], shift_ref[...]).astype(jnp.bfloat16)

    for copy in partials:
        copy.wait_send()
    for pos in (1, 2, 3):
        token_copies[pos].wait_send()
    for copy in weight_copies:
        copy.wait_send()


def vmem():
    return pl.BlockSpec(memory_space=pltpu.VMEM)


def on_device(
    queries, keys, values, layer_input, lengths, groups, prefix_keys, prefix_values,
    up_weight, up_bias, down_weight, down_bias, attn_gain, attn_shift, out_gain, out_shift,
):
    slots, width = queries.shape
    heads = width // HD
    plen = prefix_keys.shape[1]
    rows = GRP * CAP
    local = up_bias.shape[0]
    odd = lax.rem(lax.axis_index("z"), 2)
    bias_line = up_bias.astype(jnp.float32)[None]
    blank = jnp.zeros_like(bias_line)
    bias_line = jnp.concatenate(
        [jnp.where(odd == 0, bias_line, blank), jnp.where(odd == 0, blank, bias_line)], axis=1
    )
    up_half = lax.all_gather(up_weight, ("x", "z"), axis=1, tiled=True)
    down_half = lax.all_gather(down_weight, ("x", "z"), axis=0, tiled=True)
    f32, bf16 = jnp.float32, jnp.bfloat16
    dma = pltpu.SemaphoreType.DMA
    smem = pl.BlockSpec(memory_space=pltpu.SMEM)
    hidden_state, bias_all = pl.pallas_call(
        prefix_kernel,
        out_shape=(
            jax.ShapeDtypeStruct((slots, width), bf16),
            jax.ShapeDtypeStruct((NC, DEV * local), f32),
        ),
        in_specs=[smem, smem] + [vmem()] * 9,
        out_specs=(vmem(), vmem()),
        scratch_shapes=[
            pltpu.VMEM((GRP * DEV, CAP, HD), bf16),
            pltpu.VMEM((GRP * DEV, CAP, HD), bf16),
            pltpu.VMEM((GRP * DEV, CAP, HD), bf16),
            pltpu.VMEM((GRP * DEV, CAP, HD), bf16),
            pltpu.VMEM((GRP * DEV, 1, HD), f32),
            pltpu.VMEM((GRP * DEV, 1, HD), f32),
            pltpu.VMEM((NC * DEV, 1, HD), f32),
            pltpu.VMEM((rows, plen), f32),
            pltpu.VMEM((rows, plen), f32),
            pltpu.VMEM((rows, plen), bf16),
            pltpu.VMEM((rows, plen), bf16),
            pltpu.VMEM((rows, HD), f32),
            pltpu.VMEM((2, rows, 1), f32),
            pltpu.VMEM((2, rows, 1), f32),
            pltpu.VMEM((slots, width), f32),
            pltpu.VMEM((heads, slots, 1), f32),
            pltpu.VMEM((heads, slots, 1), f32),
            dma, dma((DEV,)), dma, dma, dma, dma, dma, dma, dma((4,)),
        ],
        compiler_params=pltpu.CompilerParams(collective_id=0, has_side_effects=True, vmem_limit_bytes=LIMIT),
        cost_estimate=pl.CostEstimate(flops=20_000_000_000, bytes_accessed=8_000_000, transcendentals=17_000_000),
        name="prefix",
    )(
        lengths, groups, queries, keys, values, layer_input, bias_line,
        prefix_keys[0], prefix_values[0], attn_gain[None], attn_shift[None],
    )
    units = DEV * local
    anywhere = pl.BlockSpec(memory_space=pl.ANY)
    return pl.pallas_call(
        mlp_kernel,
        out_shape=jax.ShapeDtypeStruct((slots, width), bf16),
        in_specs=[vmem(), vmem(), anywhere, anywhere, vmem(), vmem(), vmem()],
        out_specs=vmem(),
        scratch_shapes=[
            pltpu.VMEM((NY * slots, width), bf16),
            pltpu.VMEM((NC, width, units), bf16),
            pltpu.VMEM((NC, units, width), bf16),
            pltpu.VMEM((NY * slots, units), bf16),
            pltpu.VMEM((NY * slots, width), f32),
            pltpu.VMEM((3, slots, width), bf16),
            pltpu.VMEM((3, slots, width), bf16),
            dma((2,)), dma((2,)), dma((2,)), dma((3,)), dma((3,)), dma((3,)), dma((3,)),
        ],
        compiler_params=pltpu.CompilerParams(collective_id=1, has_side_effects=True, vmem_limit_bytes=LIMIT),
        name="mlp",
    )(hidden_state, bias_all, up_half, down_half, down_bias[None], out_gain[None], out_shift[None])


def solution(mesh):
    fine = Mesh(mesh.devices.reshape(NY, NC, NX, NZ), ("y", "c", "x", "z"))
    grp, dev = ("y", "c"), ("x", "z")
    every = grp + dev
    token_rows = P(every, None)
    placed = (
        (token_rows,) * 6
        + (P(grp, None, dev),) * 2
        + (P(None, every), P(every), P(every, None))
        + (P(),) * 5
    )
    return jax.shard_map(on_device, mesh=fine, in_specs=placed, out_specs=token_rows, check_vma=False)
```

time: 414 us -> 211 us (0.51)
  Pallas kernels: 0 us -> 151 us
  waiting for transfers between devices: 184 us -> 36.7 us
  local copies, waits for them, and re-layouts: 69.7 us -> 8.34 us
  matrix products: 46.3 us -> 0 us
  between operations: 44.2 us -> 13.4 us
  other arithmetic: 28.4 us -> 1.25 us
  starting transfers between devices: 25.6 us -> 0.04 us
  blocking collectives: 13.3 us -> 0 us
    pallas_call x0 -> x2, Pallas kernels: none -> 151 us  [the longest x1 86 us: on_device(): pl.pallas_call(prefix_kernel, out_shape=(jax.ShapeDtypeStruct((slots, wid...]
    reduce_scatter x1 -> x0, waiting for transfers between devices: 83.7 us -> none  [on_device(): lax.psum_scatter(jnp.dot(activation, down_slice, preferred_element_type=j...]
    dynamic_update_slice x48 -> x0, local copies, waits for them, and re-layouts: 51.1 us -> none  [the longest x8 40.9 us: on_device(): lax.dynamic_update_slice(placed_answer, own_answer, (starts[request], anc...]
    all_to_all x4 -> x0, waiting for transfers between devices: 46.6 us -> none  [the longest x1 17.8 us: on_device(): lax.all_to_all(outgoing.reshape(group_count * column_count, capacity, par...]
    dot_general x19 -> x0, matrix products: 46.3 us -> none  [the longest x8 17.2 us: one_block(): jnp.einsum('hqk,khd->qhd', weights.astype(jnp.bfloat16), value_heads, pre...]
    all_to_all x4 -> x0, starting transfers between devices: 25.5 us -> none  [the longest x1 11.6 us: on_device(): lax.all_to_all(outgoing.reshape(group_count * column_count, capacity, par...]
    all_gather x3 -> x2, waiting for transfers between devices: 52.4 us -> 35.3 us  [the longest x1 35.3 us: on_device(): down_half = lax.all_gather(down_weight, ('x', 'z'), axis=0, tiled=True)]
    reduce_sum x14 -> x0, other arithmetic: 15.4 us -> none  [the longest x8 12 us: one_block(): row_sum = jnp.sum(weights, axis=2)]
  transfers between devices with their start and end apart: 8 -> 2, of which waited for: 6 -> 1; matrix products, arithmetic and copies ran while one was open for 30% -> 4% of each run, Pallas kernels for 0% -> 41%
where the time goes in v1:
time: 211 us
  Pallas kernels  151 us (72%)
  waiting for transfers between devices  36.7 us (17%)
  between operations  13.4 us (6%)
  local copies, waits for them, and re-layouts  8.34 us (4%)
    pallas_call x1, Pallas kernels, on_device(): pl.pallas_call(prefix_kernel, out_shape=(jax.ShapeDtypeStruct((slots, wid...  86 us
    pallas_call x1, Pallas kernels, on_device(): pl.pallas_call(mlp_kernel, out_shape=jax.ShapeDtypeStruct((slots, width),...  65.2 us
    all_gather x1, waiting for transfers between devices, on_device(): down_half = lax.all_gather(down_weight, ('x', 'z'), axis=0, tiled=True)  35.3 us
    all_gather x1, local copies, waits for them, and re-layouts, on_device(): up_half = lax.all_gather(up_weight, ('x', 'z'), axis=1, tiled=True)  6.46 us
  transfers between devices with their start and end apart: 2, of which 1 were waited for; matrix products, arithmetic and copies ran while one was open for 4% of the time, Pallas kernels for 41%

profile of v1, /device:TPU:1, one launch (start us, length us, event | category | flops | bytes accessed | tf_op | source)
XLA Modules:
  0.0 211.0 jit_solution(18353521377300255610)
XLA Ops:
  6.5 0.0 all-gather.3.cloned.1.call-start
  6.5 0.7 all-gather.3.cloned.1.call-update
  7.3 0.0 all-gather.5.cloned.1.call-start
  7.3 0.7 all-gather.5.cloned.1.call-update
  8.0 0.7 fusion
  8.7 0.6 pad_maximum_fusion.bias_ref
  9.3 86.0 %prefix.1 = (bf16[128,2048]{1,0:T(8,128)(2,1)}, f32[2,1024]{1,0:T(2,128)}) custom-call(s32[1,8]{1,0:T(1,128)} %len_ref.1, s32[1,8]{1,0:T(1,128)} %grp_ref.1, bf16[128,2048]{1,0:T(8,128)(2,1)} %q_ref.1, bf16[128,2048]{1,0:T(8,128)(2,1)} %k_ref.1, bf16[128,2048]{1,0:T(8,128)(2,1)} %v_ref.1, bf16[128,2048]{1,0:T(8,128)(2,1)} %x_ref.1, ...), custom_call_target="tpu_custom_call" | custom-call | flops 20000000000 | bytes 8000000 | tf_op jit(solution)/shard_map/prefix/pallas_call | solution.py:432
  95.3 0.0 all-gather.3.cloned.1.call-done
  95.3 6.5 %copy.18.up_ref = bf16[2048,1024]{1,0:T(8,128)(2,1)} copy(bf16[2048,1024]{0,1:T(8,128)(2,1)} %all-gather.3.cloned.1.call-done) | data formatting | bytes 8388608 | tf_op jit(solution)/shard_map/all_gather | solution.py:427
  101.8 35.3 %all-gather.5.cloned.1.call-done.down_ref = bf16[1024,2048]{1,0:T(8,128)(2,1)} async-done(((bf16[64,2048]{1,0:T(8,128)(2,1)}), bf16[1024,2048]{1,0:T(8,128)(2,1)}) %all-gather.5.cloned.1.call-update) | async-done | bytes 4194320 | tf_op jit(solution)/shard_map/all_gather | solution.py:428
  137.0 65.2 %mlp.1 = bf16[128,2048]{1,0:T(8,128)(2,1)} custom-call(bf16[128,2048]{1,0:T(8,128)(2,1)} %get-tuple-element.7.hid_ref, f32[2,1024]{1,0:T(2,128)} %get-tuple-element.8.bias_ref, bf16[2048,1024]{1,0:T(8,128)(2,1)} %copy.18.up_ref, bf16[1024,2048]{1,0:T(8,128)(2,1)} %all-gather.5.cloned.1.call-done.down_ref, f32[1,2048]{1,0:T(1,128)} %bitcast.11, ...), custom_call_target="tpu_custom_call" | custom-call | tf_op jit(solution)/shard_map/mlp/pallas_call | solution.py:469
  202.3 1.9 copy.20
Async XLA Ops:
  6.5 88.8 %all-gather.3.cloned.1.call-start = ((), (), s32[]{:S(2)}) async-start(), calls=%async_computation | async-start | bytes 4456448 | tf_op jit(solution)/shard_map/all_gather | solution.py:427
  7.3 129.8 %all-gather.5.cloned.1.call-start = ((), (), s32[]{:S(2)}) async-start(), calls=%async_computation.1 | async-start | bytes 4456448 | tf_op jit(solution)/shard_map/all_gather | solution.py:428
Sparse Core Ops, SparseCore 0:
  9.5 72.5 all-gather.2
  84.2 52.7 all-gather.4

commit v2 on v1

v2 whole, which is shorter than its diff:
```python
import functools

import jax
import jax.numpy as jnp
from jax import lax
from jax.experimental import pallas as pl
from jax.experimental.pallas import tpu as pltpu
from jax.sharding import Mesh, PartitionSpec as P

HD = 128
NY, NC, NX, NZ = 4, 2, 4, 4
GRP, DEV = NY * NC, NX * NZ
CAP = 32
LOG2E = 1.4426950408889634
SCALE2 = HD**-0.5 * LOG2E
NORM_EPS = 1e-12
NEG = -1e30
MESH = pl.DeviceIdType.MESH
NT_DIMS = (((1,), (1,)), ((), ()))
LIMIT = 64 * 1024 * 1024 - 65536


def coordinates():
    return tuple(lax.axis_index(name) for name in ("y", "c", "x", "z"))


def place(y, c, x, z):
    return {"y": y, "c": c, "x": x, "z": z}


def plane_at(x, z, block):
    return lax.rem(x + block // NZ, NX), lax.rem(z + lax.rem(block, NZ), NZ)


def plane_back(x, z, block):
    return lax.rem(x + NX - block // NZ, NX), lax.rem(z + NZ - lax.rem(block, NZ), NZ)


def block_index(x, z, c):
    return z * (NC * NX) + c * NX + x


def wait_bytes(ref, sem):
    pltpu.make_async_copy(ref, ref, sem).wait()


def norm_rows(summed, gain, shift):
    mean = jnp.mean(summed, axis=-1, keepdims=True)
    centred = summed - mean
    spread = jnp.mean(centred * centred, axis=-1, keepdims=True)
    return centred * lax.rsqrt(spread + NORM_EPS) * gain + shift


def slot_tables(len_ref, grp_ref, shape, dim):
    slot = lax.broadcasted_iota(jnp.int32, shape, dim)
    start = jnp.int32(0)
    group = jnp.zeros(shape, jnp.int32)
    rank = jnp.zeros(shape, jnp.int32)
    for request in range(len_ref.shape[1]):
        length = len_ref[0, request]
        inside = (slot >= start) & (slot < start + length)
        group = jnp.where(inside, grp_ref[0, request], group)
        rank = jnp.where(inside, slot - start, rank)
        start = start + length
    return group, rank


def layer_kernel(
    len_ref, grp_ref, q_ref, bias_ref, k_in, v_in, x_in, pk_in, pv_in, up_in, down_in,
    again_ref, ashift_ref, dbias_ref, ogain_ref, oshift_ref,
    out_ref,
    k_ref, v_ref, x_ref, pk_ref, pv_ref,
    qs, qr, ans_s, ans_r, lse_s, lse_r, bias_s, bias_r, bias_all,
    s0, s1, p0, p1, acc, peak, tops, sums, mixed, own_top, own_sum,
    wu, wd, tok, hidden, total_acc, half_s, half_r, part_s, part_r,
    q_send, q_recv, a_send, a_recv, l_send, l_recv, b_send, b_recv, self_sem, in_sem,
    w_send, w_recv, w_cross, t_send, t_recv, h_send, h_recv, p_send, p_recv,
):
    y, c, x, z = coordinates()
    me_g = y * NC + c
    me_d = x * NZ + z
    slots = q_ref.shape[0]
    heads = q_ref.shape[1] // HD
    s_bufs, p_bufs = (s0, s1), (p0, p1)
    rows = GRP * CAP
    plen = pk_ref.shape[0]

    def group_at(k):
        g = lax.rem(me_g + k, GRP)
        return g, g // NC, lax.rem(g, NC)

    loads = [
        pltpu.make_async_copy(src, dst, in_sem.at[n])
        for n, (src, dst) in enumerate(
            ((k_in, k_ref), (v_in, v_ref), (pk_in, pk_ref), (pv_in, pv_ref), (x_in, x_ref))
        )
    ]
    for load in loads:
        load.start()
    barrier = pltpu.get_barrier_semaphore()

    def greet(block, k):
        tx, tz = plane_at(x, z, block)
        _, ty, tc = group_at(k)
        pl.semaphore_signal(barrier, inc=1, device_id=place(ty, tc, tx, tz), device_id_type=MESH)

    for k in range(1, GRP):
        greet(0, k)

    @pl.loop(1, DEV)
    def _(block):
        for k in range(GRP):
            greet(block, k)

    group_row, rank_row = slot_tables(len_ref, grp_ref, (1, slots), 1)
    pick = lax.broadcasted_iota(jnp.int32, (rows, slots), 0) == group_row * CAP + rank_row
    pick = pick.astype(jnp.float32).astype(jnp.bfloat16)
    line = bias_ref[...].astype(jnp.float32)
    line = jnp.concatenate([line, line], axis=1)
    side = lax.broadcasted_iota(jnp.int32, line.shape, 1) // (HD // 2)
    bias_s[...] = jnp.where(side == lax.rem(x, 2), line, 0.0)
    for d in range(heads):
        packed = jnp.dot(pick, q_ref[:, d * HD : (d + 1) * HD], preferred_element_type=jnp.float32)
        packed = packed.astype(jnp.bfloat16).reshape(GRP, CAP, HD)
        for g in range(GRP):
            qs[g * DEV + d] = packed[g]
    pl.semaphore_wait(barrier, GRP * DEV - 1)

    weights = (wu, wd)
    sources = (up_in, down_in)
    ring_steps = (0, -1, 1, 2)

    def block_of(ab, r1, r2, core):
        rx, rz = (r1, r2) if ab == 0 else (r2, r1)
        return block_index(lax.rem(x + rx + NX, NX), lax.rem(z + rz + NZ, NZ), core)

    def along(ab, axis, step):
        if (ab + axis) % 2 == 0:
            return place(y, c, lax.rem(x + step + NX, NX), z)
        return place(y, c, x, lax.rem(z + step + NZ, NZ))

    partner = place(y, 1 - c, x, z)

    def weight_part(ab, r1, r2, part):
        block = weights[ab].at[block_of(ab, r1, r2, c)]
        return block if part is None else block.at[pl.ds(part * 32, 32)]

    def weight_send(ab, r1, r2, part, axis, step, phase, kind):
        dst = weight_part(ab, r1, r2, part)
        src = sources[ab] if (r1 == 0 and r2 == 0) else dst
        pltpu.make_async_remote_copy(
            src_ref=src, dst_ref=dst, send_sem=w_send.at[ab], recv_sem=w_recv.at[ab, phase, kind],
            device_id=along(ab, axis, step), device_id_type=MESH,
        ).start()

    def weight_cross(ab, r1, r2):
        block = weight_part(ab, r1, r2, None)
        src = sources[ab] if (r1 == 0 and r2 == 0) else block
        pltpu.make_async_remote_copy(
            src_ref=src, dst_ref=block, send_sem=w_send.at[ab], recv_sem=w_cross.at[ab, ring_steps.index(r2)],
            device_id=partner, device_id_type=MESH,
        ).start()

    def weight_wait(ab, phase, kind):
        ref = weights[ab].at[0]
        wait_bytes(ref if kind < 2 else ref.at[pl.ds(0, 32)], w_recv.at[ab, phase, kind])

    def first_own(ab):
        weight_send(ab, 0, 0, None, 0, 1, 0, 0)
        weight_send(ab, 0, 0, None, 0, -1, 0, 1)

    def first_direct(ab):
        weight_wait(ab, 0, 0)
        weight_send(ab, -1, 0, 0, 0, 1, 0, 2)
        weight_wait(ab, 0, 1)
        weight_send(ab, 1, 0, 1, 0, -1, 0, 3)
        weight_cross(ab, -1, 0)
        weight_cross(ab, 1, 0)

    def first_half(ab):
        weight_wait(ab, 0, 2)
        weight_wait(ab, 0, 3)
        weight_cross(ab, 2, 0)

    def second_own(ab, k):
        weight_send(ab, ring_steps[k], 0, None, 1, 1, 1 + k, 0)
        weight_send(ab, ring_steps[k], 0, None, 1, -1, 1 + k, 1)

    def second_direct(ab, k):
        r1 = ring_steps[k]
        weight_wait(ab, 1 + k, 0)
        weight_send(ab, r1, -1, 0, 1, 1, 1 + k, 2)
        weight_wait(ab, 1 + k, 1)
        weight_send(ab, r1, 1, 1, 1, -1, 1 + k, 3)
        weight_cross(ab, r1, -1)
        weight_cross(ab, r1, 1)

    def second_half(ab, k):
        weight_wait(ab, 1 + k, 2)
        weight_wait(ab, 1 + k, 3)
        weight_cross(ab, ring_steps[k], 2)

    own_weights = [
        pltpu.make_async_copy(sources[ab], weights[ab].at[block_of(ab, 0, 0, c)], in_sem.at[5 + ab])
        for ab in range(2)
    ]

    def weights_begin():
        for ab in range(2):
            own_weights[ab].start()
            first_own(ab)
            weight_cross(ab, 0, 0)
        for ab in range(2):
            second_own(ab, 0)

    def weights_1():
        for ab in range(2):
            first_direct(ab)
        for ab in range(2):
            second_own(ab, 1)
            second_own(ab, 2)

    def weights_2():
        for ab in range(2):
            second_direct(ab, 0)
            first_half(ab)
            second_own(ab, 3)

    def weights_3():
        for ab in range(2):
            second_half(ab, 0)
            second_direct(ab, 1)
            second_direct(ab, 2)

    def weights_4():
        for ab in range(2):
            second_direct(ab, 3)

    def weights_5(ab):
        for k in (1, 2, 3):
            second_half(ab, k)

    def cross_wait(ab, r2):
        wait_bytes(weights[ab].at[pl.ds(0, 4)], w_cross.at[ab, ring_steps.index(r2)])

    def send_query(block, k):
        tx, tz = plane_at(x, z, block)
        g, ty, tc = group_at(k)
        pltpu.make_async_remote_copy(
            src_ref=qs.at[g * DEV + tx * NZ + tz],
            dst_ref=qr.at[block * GRP + me_g],
            send_sem=q_send,
            recv_sem=q_recv.at[block],
            device_id=place(ty, tc, tx, tz),
            device_id_type=MESH,
        ).start()

    own_query = pltpu.make_async_copy(qs.at[me_g * DEV + me_d], qr.at[me_g], self_sem.at[0])
    own_query.start()
    for k in range(1, GRP):
        send_query(0, k)

    @pl.loop(1, DEV)
    def _(block):
        for k in range(GRP):
            send_query(block, k)

    for k in range(1, NC * DEV):
        tc = lax.rem(c + k // DEV, NC)
        tx, tz = plane_at(x, z, k % DEV)
        pltpu.make_async_remote_copy(
            src_ref=bias_s,
            dst_ref=bias_r.at[block_index(x, z, c)],
            send_sem=b_send,
            recv_sem=b_recv,
            device_id=place(y, tc, tx, tz),
            device_id_type=MESH,
        ).start()
    own_bias = pltpu.make_async_copy(bias_s, bias_r.at[block_index(x, z, c)], self_sem.at[3])
    own_bias.start()
    weights_begin()
    loads[0].wait()
    loads[1].wait()

    group_col, rank_col = slot_tables(len_ref, grp_ref, (slots, 1), 0)
    visible = (group_col == group_row) & (
        lax.broadcasted_iota(jnp.int32, (slots, slots), 1)
        <= lax.broadcasted_iota(jnp.int32, (slots, slots), 0)
    )

    @pl.loop(0, heads)
    def _(h):
        cols = pl.ds(pl.multiple_of(h * HD, HD), HD)
        s = lax.dot_general(q_ref[:, cols], k_ref[:, cols], NT_DIMS, preferred_element_type=jnp.float32)
        s = jnp.where(visible, s * SCALE2, NEG)
        top = jnp.max(s, axis=1, keepdims=True)
        w = jnp.where(visible, jnp.exp2(s - top), 0.0)
        own_top[h] = top
        own_sum[h] = jnp.sum(w, axis=1, keepdims=True)
        mixed[:, cols] = jnp.dot(w.astype(jnp.bfloat16), v_ref[:, cols], preferred_element_type=jnp.float32)

    def answer_back(block, k):
        tx, tz = plane_back(x, z, block)
        g, ty, tc = group_at(k)
        where = place(ty, tc, tx, tz)
        pltpu.make_async_remote_copy(
            src_ref=ans_s.at[block * GRP + g],
            dst_ref=ans_r.at[me_d * GRP + me_g],
            send_sem=a_send, recv_sem=a_recv, device_id=where, device_id_type=MESH,
        ).start()
        pltpu.make_async_remote_copy(
            src_ref=lse_s.at[block * GRP + g],
            dst_ref=lse_r.at[me_d * GRP + me_g],
            send_sem=l_send, recv_sem=l_recv, device_id=where, device_id_type=MESH,
        ).start()

    steps = 4
    span = plen // steps
    part = rows // steps

    def stage(i, parity, scoring, weighing, mixing, first=False):
        other = 1 - parity
        if scoring:
            if first:
                wait_bytes(qr.at[pl.ds(0, GRP - 1)], q_recv.at[0])
                own_query.wait()
            else:
                wait_bytes(qr.at[pl.ds(i * GRP, GRP)], q_recv.at[i])
            peak[...] = jnp.full_like(peak, NEG)
        if mixing:
            acc[...] = jnp.zeros_like(acc)

        @pl.loop(0, steps)
        def _(j):
            keys = pl.ds(pl.multiple_of(j * span, span), span)
            if scoring:
                block = qr[pl.ds(i * GRP, GRP)].reshape(rows, HD)
                s = lax.dot_general(block, pk_ref[keys, :], NT_DIMS, preferred_element_type=jnp.float32)
                s_bufs[parity][:, keys] = s
                high = s[:, :HD]
                for t in range(1, span // HD):
                    high = jnp.maximum(high, s[:, t * HD : (t + 1) * HD])
                peak[...] = jnp.maximum(peak[...], high)
            if weighing:
                some = pl.ds(pl.multiple_of(j * part, part), part)
                top = tops[other, some, :]
                total = jnp.zeros((part, HD), jnp.float32)
                for t in range(plen // HD):
                    cols = slice(t * HD, (t + 1) * HD)
                    w = jnp.exp2(s_bufs[other][some, cols] * SCALE2 - top)
                    total = total + w
                    p_bufs[other][some, cols] = w.astype(jnp.bfloat16)
                sums[other, some, :] = total
            if mixing:
                acc[...] += jnp.dot(p_bufs[parity][:, keys], pv_ref[keys, :], preferred_element_type=jnp.float32)

        if mixing:
            done = i - 2
            total = jnp.sum(sums[parity], axis=1, keepdims=True)
            answer = (acc[...] / total).astype(jnp.bfloat16).reshape(GRP, CAP, HD)
            spread = (tops[parity] + jnp.log(total) * LOG2E).reshape(GRP, CAP, HD)
            diagonal = lax.broadcasted_iota(jnp.int32, (GRP, CAP, HD), 1) == lax.broadcasted_iota(
                jnp.int32, (GRP, CAP, HD), 2
            )
            lines = jnp.sum(jnp.where(diagonal, spread, 0.0), axis=1)
            for g in range(GRP):
                ans_s[done * GRP + g] = answer[g]
                lse_s[done * GRP + g] = lines[g : g + 1]
        if scoring:
            tops[parity] = jnp.broadcast_to(jnp.max(peak[...], axis=1, keepdims=True) * SCALE2, (rows, HD))

    def send_back(done):
        for k in range(GRP):
            answer_back(done, k)

    loads[2].wait()
    loads[3].wait()
    stage(0, 0, True, False, False, first=True)
    stage(1, 1, True, True, False)
    stage(2, 0, True, True, True)
    own_answer = pltpu.make_async_copy(ans_s.at[me_g], ans_r.at[me_d * GRP + me_g], self_sem.at[1])
    own_lse = pltpu.make_async_copy(lse_s.at[me_g], lse_r.at[me_d * GRP + me_g], self_sem.at[2])
    own_answer.start()
    own_lse.start()
    for k in range(1, GRP):
        answer_back(0, k)
    stage(3, 1, True, True, True)
    send_back(1)

    def stage_pairs(first_pair, last_pair):
        @pl.loop(first_pair, last_pair)
        def _(pair):
            stage(2 * pair, 0, True, True, True)
            send_back(2 * pair - 2)
            stage(2 * pair + 1, 1, True, True, True)
            send_back(2 * pair - 1)

    stage_pairs(2, 4)
    weights_1()
    stage_pairs(4, 6)
    weights_2()
    stage_pairs(6, 8)
    weights_3()
    stage(DEV, 0, False, True, True)
    send_back(DEV - 2)
    stage(DEV + 1, 1, False, False, True)
    send_back(DEV - 1)

    own_bias.wait()
    wait_bytes(bias_r.at[pl.ds(0, NC * DEV - 1)], b_recv)
    for e in range(NC * DEV // 2):
        bias_all[:, e * HD : (e + 1) * HD] = bias_r[2 * e] + bias_r[2 * e + 1]

    weights_4()
    own_answer.wait()
    own_lse.wait()
    wait_bytes(ans_r.at[pl.ds(0, GRP * DEV - 1)], a_recv)
    wait_bytes(lse_r.at[pl.ds(0, GRP * DEV - 1)], l_recv)
    unpick = lax.broadcasted_iota(jnp.int32, (slots, rows), 1) == group_col * CAP + rank_col
    unpick = unpick.astype(jnp.float32).astype(jnp.bfloat16)
    lane = lax.broadcasted_iota(jnp.int32, (slots, HD), 1)

    @pl.loop(0, heads)
    def _(h):
        cols = pl.ds(pl.multiple_of(h * HD, HD), HD)
        far = jnp.dot(
            unpick, ans_r[pl.ds(h * GRP, GRP)].reshape(rows, HD), preferred_element_type=jnp.float32
        )
        spread = jnp.zeros((slots, HD), jnp.float32)
        for g in range(GRP):
            spread = jnp.where(group_col == g, lse_r[h * GRP + g], spread)
        far_top = jnp.sum(jnp.where(lane == rank_col, spread, 0.0), axis=1, keepdims=True)
        top = own_top[h]
        joint = jnp.maximum(far_top, top)
        far_weight = jnp.exp2(far_top - joint)
        own_weight = jnp.exp2(top - joint)
        below = far_weight + own_weight * own_sum[h]
        mixed[:, cols] = (far_weight * far + own_weight * mixed[:, cols]) / below

    loads[4].wait()

    @pl.loop(0, slots // 16)
    def _(r):
        some = pl.ds(pl.multiple_of(r * 16, 16), 16)
        summed = x_ref[some, :].astype(jnp.float32) + mixed[some, :]
        tok[some, :] = norm_rows(summed, again_ref[...], ashift_ref[...]).astype(jnp.bfloat16)

    def y_copy(src, dst, send_sem, recv_sem, step):
        return pltpu.make_async_remote_copy(
            src_ref=src, dst_ref=dst, send_sem=send_sem, recv_sem=recv_sem,
            device_id=place(lax.rem(y + step + NY, NY), c, x, z), device_id_type=MESH,
        )

    def token(pos, part=None):
        return tok.at[pl.ds(pos * slots, slots)] if part is None else tok.at[
            pl.ds(pos * slots + part * (slots // 2), slots // 2)
        ]

    sent = [
        y_copy(token(0), token(2), t_send.at[0], t_recv.at[0], 1),
        y_copy(token(0), token(1), t_send.at[1], t_recv.at[1], -1),
    ]
    sent[0].start()
    sent[1].start()
    own_weights[0].wait()
    own_weights[1].wait()
    width = q_ref.shape[1]
    tile = 256
    per_tile = tile // 64

    def up(first, count, r2):
        rows_ = pl.ds(first * slots, count * slots)
        base = lax.rem(z + r2 + NZ, NZ) * (NC * NX)

        @pl.loop(0, NC * NX // per_tile)
        def _(n):
            block = base + n * per_tile
            cols = pl.ds(pl.multiple_of(block * 64, tile), tile)
            u = lax.dot_general(
                tok[rows_, :], wu[pl.ds(block, per_tile)].reshape(tile, width), NT_DIMS,
                preferred_element_type=jnp.float32,
            )
            u = u + bias_all[:, cols]
            hidden[rows_, cols] = jax.nn.gelu(u, approximate=True).astype(jnp.bfloat16)

    def down(first, count):
        rows_ = pl.ds(first * slots, count * slots)

        @pl.loop(0, width // tile)
        def _(n):
            cols = pl.ds(pl.multiple_of(n * tile, tile), tile)
            total_acc[rows_, cols] = jnp.dot(
                hidden[rows_, :], wd[:, :, cols].reshape(NC * DEV * 64, tile),
                preferred_element_type=jnp.float32,
            )

    cross_wait(0, 0)
    up(0, 1, 0)
    wait_bytes(token(2), t_recv.at[0])
    wait_bytes(token(1), t_recv.at[1])
    sent.append(y_copy(token(2, 0), token(3, 0), t_send.at[2], t_recv.at[2], 1))
    sent.append(y_copy(token(1, 1), token(3, 1), t_send.at[3], t_recv.at[3], -1))
    sent[2].start()
    sent[3].start()
    weights_5(0)
    weights_5(1)
    for r2 in ring_steps[1:]:
        cross_wait(0, r2)
        up(0, 1, r2)
    for r2 in ring_steps:
        up(1, 2, r2)
    wait_bytes(token(3, 0), t_recv.at[2])
    wait_bytes(token(3, 1), t_recv.at[3])
    for r2 in ring_steps:
        up(3, 1, r2)
    for r2 in ring_steps:
        cross_wait(1, r2)
    down(3, 1)
    cut = width // 2
    for side in range(2):
        half_s[side] = total_acc[3 * slots :, side * cut : (side + 1) * cut].astype(jnp.bfloat16)
        sent.append(y_copy(half_s.at[side], half_r.at[side], h_send.at[side], h_recv.at[side], 1 - 2 * side))
        sent[-1].start()
    down(1, 2)
    for side in range(2):
        wait_bytes(half_r.at[side], h_recv.at[side])
        at = slice((1 + side) * slots, (2 + side) * slots)
        for half in range(2):
            cols = slice(half * cut, (half + 1) * cut)
            partial = total_acc[at, cols]
            if half == side:
                partial = partial + half_r[side].astype(jnp.float32)
            part_s[side, :, cols] = partial.astype(jnp.bfloat16)
        sent.append(y_copy(part_s.at[side], part_r.at[side], p_send.at[side], p_recv.at[side], 1 - 2 * side))
        sent[-1].start()
    down(0, 1)
    for side in range(2):
        wait_bytes(part_r.at[side], p_recv.at[side])

    @pl.loop(0, slots // 16)
    def _(r):
        some = pl.ds(pl.multiple_of(r * 16, 16), 16)
        total = total_acc[some, :] + tok[some, :].astype(jnp.float32) + dbias_ref[...]
        for side in range(2):
            total = total + part_r[side, some, :].astype(jnp.float32)
        out_ref[some, :] = norm_rows(total, ogain_ref[...], oshift_ref[...]).astype(jnp.bfloat16)

    for copy in sent:
        copy.wait_send()
    wait_bytes(qs.at[pl.ds(0, GRP * DEV - 1)], q_send)
    wait_bytes(ans_s.at[pl.ds(0, GRP * DEV - 1)], a_send)
    wait_bytes(lse_s.at[pl.ds(0, GRP * DEV - 1)], l_send)
    wait_bytes(bias_r.at[pl.ds(0, NC * DEV - 1)], b_send)
    for ab in range(2):
        wait_bytes(weights[ab].at[pl.ds(0, NC * DEV - 1)], w_send.at[ab])


def vmem():
    return pl.BlockSpec(memory_space=pltpu.VMEM)


def on_device(
    queries, keys, values, layer_input, lengths, groups, prefix_keys, prefix_values,
    up_weight, up_bias, down_weight, down_bias, attn_gain, attn_shift, out_gain, out_shift,
):
    slots, width = queries.shape
    heads = width // HD
    plen = prefix_keys.shape[1]
    rows = GRP * CAP
    local = up_bias.shape[0]
    units = NC * DEV * local
    f32, bf16 = jnp.float32, jnp.bfloat16
    dma = pltpu.SemaphoreType.DMA
    smem = pl.BlockSpec(memory_space=pltpu.SMEM)
    anywhere = pl.BlockSpec(memory_space=pl.ANY)
    messages = pltpu.VMEM((GRP * DEV, CAP, HD), bf16)
    lines = pltpu.VMEM((GRP * DEV, 1, HD), f32)
    return pl.pallas_call(
        layer_kernel,
        out_shape=jax.ShapeDtypeStruct((slots, width), bf16),
        in_specs=[smem] * 2 + [vmem()] * 2 + [anywhere] * 7 + [vmem()] * 5,
        out_specs=vmem(),
        scratch_shapes=[
            pltpu.VMEM((slots, width), bf16),
            pltpu.VMEM((slots, width), bf16),
            pltpu.VMEM((slots, width), bf16),
            pltpu.VMEM((plen, HD), bf16),
            pltpu.VMEM((plen, HD), bf16),
            messages, messages, messages, messages, lines, lines,
            pltpu.VMEM((1, HD), f32),
            pltpu.VMEM((NC * DEV, 1, HD), f32),
            pltpu.VMEM((1, units), f32),
            pltpu.VMEM((rows, plen), f32),
            pltpu.VMEM((rows, plen), f32),
            pltpu.VMEM((rows, plen), bf16),
            pltpu.VMEM((rows, plen), bf16),
            pltpu.VMEM((rows, HD), f32),
            pltpu.VMEM((rows, HD), f32),
            pltpu.VMEM((2, rows, HD), f32),
            pltpu.VMEM((2, rows, HD), f32),
            pltpu.VMEM((slots, width), f32),
            pltpu.VMEM((heads, slots, 1), f32),
            pltpu.VMEM((heads, slots, 1), f32),
            pltpu.VMEM((NC * DEV, local, width), bf16),
            pltpu.VMEM((NC * DEV, local, width), bf16),
            pltpu.VMEM((NY * slots, width), bf16),
            pltpu.VMEM((NY * slots, units), bf16),
            pltpu.VMEM((NY * slots, width), f32),
            pltpu.VMEM((2, slots, width // 2), bf16),
            pltpu.VMEM((2, slots, width // 2), bf16),
            pltpu.VMEM((2, slots, width), bf16),
            pltpu.VMEM((2, slots, width), bf16),
            dma, dma((DEV,)), dma, dma, dma, dma, dma, dma, dma((4,)), dma((7,)),
            dma((2,)), dma((2, 5, 4)), dma((2, 4)), dma((4,)), dma((4,)), dma((2,)), dma((2,)), dma((2,)), dma((2,)),
        ],
        compiler_params=pltpu.CompilerParams(collective_id=0, has_side_effects=True, vmem_limit_bytes=LIMIT),
        name="layer",
    )(
        lengths, groups, queries, up_bias[None], keys, values, layer_input,
        prefix_keys[0], prefix_values[0], up_weight.T, down_weight,
        attn_gain[None], attn_shift[None], down_bias[None], out_gain[None], out_shift[None],
    )


def solution(mesh):
    fine = Mesh(mesh.devices.reshape(NY, NC, NX, NZ), ("y", "c", "x", "z"))
    grp, dev = ("y", "c"), ("x", "z")
    every = grp + dev
    token_rows = P(every, None)
    placed = (
        (token_rows,) * 6
        + (P(grp, None, dev),) * 2
        + (P(None, every), P(every), P(every, None))
        + (P(),) * 5
    )
    return jax.shard_map(on_device, mesh=fine, in_specs=placed, out_specs=token_rows, check_vma=False)
```

time: 211 us -> 144 us (0.68)
  waiting for transfers between devices: 36.7 us -> 0 us
  between operations: 13.4 us -> 0.01 us
  Pallas kernels: 151 us -> 142 us
  local copies, waits for them, and re-layouts: 8.34 us -> 1.88 us
    all_gather x2 -> x0, waiting for transfers between devices: 35.3 us -> none  [the longest x1 35.3 us: on_device(): down_half = lax.all_gather(down_weight, ('x', 'z'), axis=0, tiled=True)]
    pallas_call x2 -> x1, Pallas kernels: 151 us -> 142 us  [on_device(): pl.pallas_call(layer_kernel, out_shape=jax.ShapeDtypeStruct((slots, width...]
    all_gather x1 -> x0, local copies, waits for them, and re-layouts: 6.46 us -> none  [on_device(): up_half = lax.all_gather(up_weight, ('x', 'z'), axis=1, tiled=True)]
  transfers between devices with their start and end apart: 2 -> 0, of which waited for: 1 -> 0; matrix products, arithmetic and copies ran while one was open for 4% -> 0% of each run, Pallas kernels for 41% -> 0%
where the time goes in v2:
time: 144 us; the launch traced here: 143 us
  Pallas kernels  142 us (99%)
  local copies, waits for them, and re-layouts  1.88 us (1%)
    pallas_call x1, Pallas kernels, on_device(): pl.pallas_call(layer_kernel, out_shape=jax.ShapeDtypeStruct((slots, width...  142 us

profile of v2, /device:TPU:1, one launch (start us, length us, event | category | flops | bytes accessed | tf_op | source)
XLA Modules:
  0.0 143.5 jit_solution(8042720651756653084)
XLA Ops:
  0.0 141.6 %layer.1 = bf16[128,2048]{1,0:T(8,128)(2,1)} custom-call(s32[1,8]{1,0:T(1,128)} %len_ref.1, s32[1,8]{1,0:T(1,128)} %grp_ref.1, bf16[128,2048]{1,0:T(8,128)(2,1)} %q_ref.1, bf16[1,64]{1,0:T(2,128)(2,1)} %bitcast.17, bf16[128,2048]{1,0:T(8,128)(2,1)} %k_in.1, bf16[128,2048]{1,0:T(8,128)(2,1)} %v_in.1, bf16[128,2048]{1,0:T(8,128)(2,1)} %x_in.1, ...), custom_call_target="tpu_custom_call" | custom-call | tf_op jit(solution)/shard_map/layer/pallas_call | solution.py:578
  141.6 1.9 %copy.18 = bf16[128,2048]{1,0:T(8,128)(2,1)} copy(bf16[128,2048]{1,0:T(8,128)(2,1)} %layer.1) | data formatting | bytes 1048576

commit v3 on v2

--- a/solution.py
+++ b/solution.py
@@ -129,119 +129,100 @@
     weights = (wu, wd)
     sources = (up_in, down_in)
     ring_steps = (0, -1, 1, 2)
-
-    def block_of(ab, r1, r2, core):
-        rx, rz = (r1, r2) if ab == 0 else (r2, r1)
-        return block_index(lax.rem(x + rx + NX, NX), lax.rem(z + rz + NZ, NZ), core)
-
-    def along(ab, axis, step):
-        if (ab + axis) % 2 == 0:
+    strip = up_in.shape[0] // 2
+
+    def block_of(q, r1, r2):
+        rx, rz = (r1, r2) if q % 2 == 0 else (r2, r1)
+        return block_index(lax.rem(x + rx + NX, NX), lax.rem(z + rz + NZ, NZ), c)
+
+    def along(q, axis, step):
+        if (q + axis) % 2 == 0:
             return place(y, c, lax.rem(x + step + NX, NX), z)
         return place(y, c, x, lax.rem(z + step + NZ, NZ))
 
     partner = place(y, 1 - c, x, z)
 
-    def weight_part(ab, r1, r2, part):
-        block = weights[ab].at[block_of(ab, r1, r2, c)]
-        return block if part is None else block.at[pl.ds(part * 32, 32)]
-
-    def weight_send(ab, r1, r2, part, axis, step, phase, kind):
-        dst = weight_part(ab, r1, r2, part)
-        src = sources[ab] if (r1 == 0 and r2 == 0) else dst
+    def strip_of(block, q, part):
+        first = (q % 2) * strip
+        if part is None:
+            return block.at[pl.ds(first, strip)]
+        return block.at[pl.ds(first + part * (strip // 2), strip // 2)]
+
+    def weight_refs(q, r1, r2, part):
+        dst = strip_of(weights[q // 2].at[block_of(q, r1, r2)], q, part)
+        src = strip_of(sources[q // 2], q, part) if (r1 == 0 and r2 == 0) else dst
+        return src, dst
+
+    def weight_send(q, r1, r2, part, axis, step, phase, kind):
+        src, dst = weight_refs(q, r1, r2, part)
         pltpu.make_async_remote_copy(
-            src_ref=src, dst_ref=dst, send_sem=w_send.at[ab], recv_sem=w_recv.at[ab, phase, kind],
-            device_id=along(ab, axis, step), device_id_type=MESH,
+            src_ref=src, dst_ref=dst, send_sem=w_send.at[q // 2], recv_sem=w_recv.at[q, phase, kind],
+            device_id=along(q, axis, step), device_id_type=MESH,
         ).start()
 
-    def weight_cross(ab, r1, r2):
-        block = weight_part(ab, r1, r2, None)
-        src = sources[ab] if (r1 == 0 and r2 == 0) else block
+    def weight_cross(q, r1, r2):
+        src, dst = weight_refs(q, r1, r2, None)
         pltpu.make_async_remote_copy(
-            src_ref=src, dst_ref=block, send_sem=w_send.at[ab], recv_sem=w_cross.at[ab, ring_steps.index(r2)],
+            src_ref=src, dst_ref=dst, send_sem=w_send.at[q // 2], recv_sem=w_cross.at[q // 2],
             device_id=partner, device_id_type=MESH,
         ).start()
 
-    def weight_wait(ab, phase, kind):
-        ref = weights[ab].at[0]
-        wait_bytes(ref if kind < 2 else ref.at[pl.ds(0, 32)], w_recv.at[ab, phase, kind])
-
-    def first_own(ab):
-        weight_send(ab, 0, 0, None, 0, 1, 0, 0)
-        weight_send(ab, 0, 0, None, 0, -1, 0, 1)
-
-    def first_direct(ab):
-        weight_wait(ab, 0, 0)
-        weight_send(ab, -1, 0, 0, 0, 1, 0, 2)
-        weight_wait(ab, 0, 1)
-        weight_send(ab, 1, 0, 1, 0, -1, 0, 3)
-        weight_cross(ab, -1, 0)
-        weight_cross(ab, 1, 0)
-
-    def first_half(ab):
-        weight_wait(ab, 0, 2)
-        weight_wait(ab, 0, 3)
-        weight_cross(ab, 2, 0)
-
-    def second_own(ab, k):
-        weight_send(ab, ring_steps[k], 0, None, 1, 1, 1 + k, 0)
-        weight_send(ab, ring_steps[k], 0, None, 1, -1, 1 + k, 1)
-
-    def second_direct(ab, k):
+    def weight_wait(q, phase, kind):
+        size = strip if kind < 2 else strip // 2
+        wait_bytes(weights[q // 2].at[0, pl.ds(0, size)], w_recv.at[q, phase, kind])
+
+    def both(tensor):
+        return (2 * tensor, 2 * tensor + 1)
+
+    def first_own(tensor):
+        for q in both(tensor):
+            weight_send(q, 0, 0, None, 0, 1, 0, 0)
+            weight_send(q, 0, 0, None, 0, -1, 0, 1)
+            weight_cross(q, 0, 0)
+
+    def first_direct(tensor):
+        for q in both(tensor):
+            weight_wait(q, 0, 0)
+            weight_send(q, -1, 0, 0, 0, 1, 0, 2)
+            weight_wait(q, 0, 1)
+            weight_send(q, 1, 0, 1, 0, -1, 0, 3)
+            weight_cross(q, -1, 0)
+            weight_cross(q, 1, 0)
+
+    def first_half(tensor):
+        for q in both(tensor):
+            weight_wait(q, 0, 2)
+            weight_wait(q, 0, 3)
+            weight_cross(q, 2, 0)
+
+    def second_own(tensor, k):
+        for q in both(tensor):
+            weight_send(q, ring_steps[k], 0, None, 1, 1, 1 + k, 0)
+            weight_send(q, ring_steps[k], 0, None, 1, -1, 1 + k, 1)
+
+    def second_direct(tensor, k):
         r1 = ring_steps[k]
-        weight_wait(ab, 1 + k, 0)
-        weight_send(ab, r1, -1, 0, 1, 1, 1 + k, 2)
-        weight_wait(ab, 1 + k, 1)
-        weight_send(ab, r1, 1, 1, 1, -1, 1 + k, 3)
-        weight_cross(ab, r1, -1)
-        weight_cross(ab, r1, 1)
-
-    def second_half(ab, k):
-        weight_wait(ab, 1 + k, 2)
-        weight_wait(ab, 1 + k, 3)
-        weight_cross(ab, ring_steps[k], 2)
+        for q in both(tensor):
+            weight_wait(q, 1 + k, 0)
+            weight_send(q, r1, -1, 0, 1, 1, 1 + k, 2)
+            weight_wait(q, 1 + k, 1)
+            weight_send(q, r1, 1, 1, 1, -1, 1 + k, 3)
+            weight_cross(q, r1, -1)
+            weight_cross(q, r1, 1)
+
+    def second_half(tensor, k):
+        for q in both(tensor):
+            weight_wait(q, 1 + k, 2)
+            weight_wait(q, 1 + k, 3)
+            weight_cross(q, ring_steps[k], 2)
+
+    def cross_wait(tensor):
+        wait_bytes(weights[tensor].at[pl.ds(0, DEV)], w_cross.at[tensor])
 
     own_weights = [
-        pltpu.make_async_copy(sources[ab], weights[ab].at[block_of(ab, 0, 0, c)], in_sem.at[5 + ab])
+        pltpu.make_async_copy(sources[ab], weights[ab].at[block_index(x, z, c)], in_sem.at[5 + ab])
         for ab in range(2)
     ]
-
-    def weights_begin():
-        for ab in range(2):
-            own_weights[ab].start()
-            first_own(ab)
-            weight_cross(ab, 0, 0)
-        for ab in range(2):
-            second_own(ab, 0)
-
-    def weights_1():
-        for ab in range(2):
-            first_direct(ab)
-        for ab in range(2):
-            second_own(ab, 1)
-            second_own(ab, 2)
-
-    def weights_2():
-        for ab in range(2):
-            second_direct(ab, 0)
-            first_half(ab)
-            second_own(ab, 3)
-
-    def weights_3():
-        for ab in range(2):
-            second_half(ab, 0)
-            second_direct(ab, 1)
-            second_direct(ab, 2)
-
-    def weights_4():
-        for ab in range(2):
-            second_direct(ab, 3)
-
-    def weights_5(ab):
-        for k in (1, 2, 3):
-            second_half(ab, k)
-
-    def cross_wait(ab, r2):
-        wait_bytes(weights[ab].at[pl.ds(0, 4)], w_cross.at[ab, ring_steps.index(r2)])
 
     def send_query(block, k):
         tx, tz = plane_at(x, z, block)
@@ -278,7 +259,10 @@
         ).start()
     own_bias = pltpu.make_async_copy(bias_s, bias_r.at[block_index(x, z, c)], self_sem.at[3])
     own_bias.start()
-    weights_begin()
+    own_weights[0].start()
+    own_weights[1].start()
+    first_own(0)
+    second_own(0, 0)
     loads[0].wait()
     loads[1].wait()
 
@@ -396,11 +380,16 @@
             send_back(2 * pair - 1)
 
     stage_pairs(2, 4)
-    weights_1()
+    first_direct(0)
+    second_own(0, 1)
+    second_own(0, 2)
     stage_pairs(4, 6)
-    weights_2()
+    second_direct(0, 0)
+    first_half(0)
+    second_own(0, 3)
     stage_pairs(6, 8)
-    weights_3()
+    second_direct(0, 1)
+    second_direct(0, 2)
     stage(DEV, 0, False, True, True)
     send_back(DEV - 2)
     stage(DEV + 1, 1, False, False, True)
@@ -411,7 +400,13 @@
     for e in range(NC * DEV // 2):
         bias_all[:, e * HD : (e + 1) * HD] = bias_r[2 * e] + bias_r[2 * e + 1]
 
-    weights_4()
+    first_own(1)
+    second_own(1, 0)
+    second_half(0, 0)
+    second_direct(0, 3)
+    first_direct(1)
+    second_own(1, 1)
+    second_own(1, 2)
     own_answer.wait()
     own_lse.wait()
     wait_bytes(ans_r.at[pl.ds(0, GRP * DEV - 1)], a_recv)
@@ -468,16 +463,14 @@
     tile = 256
     per_tile = tile // 64
 
-    def up(first, count, r2):
+    def up(first, count):
         rows_ = pl.ds(first * slots, count * slots)
-        base = lax.rem(z + r2 + NZ, NZ) * (NC * NX)
-
-        @pl.loop(0, NC * NX // per_tile)
+
+        @pl.loop(0, NC * DEV // per_tile)
         def _(n):
-            block = base + n * per_tile
-            cols = pl.ds(pl.multiple_of(block * 64, tile), tile)
+            cols = pl.ds(pl.multiple_of(n * tile, tile), tile)
             u = lax.dot_general(
-                tok[rows_, :], wu[pl.ds(block, per_tile)].reshape(tile, width), NT_DIMS,
+                tok[rows_, :], wu[pl.ds(n * per_tile, per_tile)].reshape(tile, width), NT_DIMS,
                 preferred_element_type=jnp.float32,
             )
             u = u + bias_all[:, cols]
@@ -494,55 +487,63 @@
                 preferred_element_type=jnp.float32,
             )
 
-    cross_wait(0, 0)
-    up(0, 1, 0)
+    second_direct(1, 0)
+    first_half(1)
+    second_own(1, 3)
+    for k in (1, 2, 3):
+        second_half(0, k)
+    cross_wait(0)
+    second_direct(1, 1)
+    second_direct(1, 2)
+    up(0, 1)
     wait_bytes(token(2), t_recv.at[0])
     wait_bytes(token(1), t_recv.at[1])
     sent.append(y_copy(token(2, 0), token(3, 0), t_send.at[2], t_recv.at[2], 1))
     sent.append(y_copy(token(1, 1), token(3, 1), t_send.at[3], t_recv.at[3], -1))
     sent[2].start()
     sent[3].start()
-    weights_5(0)
-    weights_5(1)
-    for r2 in ring_steps[1:]:
-        cross_wait(0, r2)
-        up(0, 1, r2)
-    for r2 in ring_steps:
-        up(1, 2, r2)
+    second_direct(1, 3)
+    up(1, 2)
     wait_bytes(token(3, 0), t_recv.at[2])
     wait_bytes(token(3, 1), t_recv.at[3])
-    for r2 in ring_steps:
-        up(3, 1, r2)
-    for r2 in ring_steps:
-        cross_wait(1, r2)
+    up(3, 1)
+    for k in range(4):
+        second_half(1, k)
+    cross_wait(1)
     down(3, 1)
     cut = width // 2
+
+    def ship(src, dst, send_sem, recv_sem, side):
+        sent.append(y_copy(src, dst, send_sem, recv_sem, 1 - 2 * side))
+        sent[-1].start()
+
     for side in range(2):
         half_s[side] = total_acc[3 * slots :, side * cut : (side + 1) * cut].astype(jnp.bfloat16)
-        sent.append(y_copy(half_s.at[side], half_r.at[side], h_send.at[side], h_recv.at[side], 1 - 2 * side))
-        sent[-1].start()
+        ship(half_s.at[side], half_r.at[side], h_send.at[side], h_recv.at[side], side)
     down(1, 2)
     for side in range(2):
+        at = slice((1 + side) * slots, (2 + side) * slots)
+        rest = 1 - side
+        part_s[side, 1] = total_acc[at, rest * cut : (rest + 1) * cut].astype(jnp.bfloat16)
+        ship(part_s.at[side, 1], part_r.at[side, 1], p_send.at[side, 1], p_recv.at[side, 1], side)
+    for side in range(2):
+        at = slice((1 + side) * slots, (2 + side) * slots)
         wait_bytes(half_r.at[side], h_recv.at[side])
-        at = slice((1 + side) * slots, (2 + side) * slots)
-        for half in range(2):
-            cols = slice(half * cut, (half + 1) * cut)
-            partial = total_acc[at, cols]
-            if half == side:
-                partial = partial + half_r[side].astype(jnp.float32)
-            part_s[side, :, cols] = partial.astype(jnp.bfloat16)
-        sent.append(y_copy(part_s.at[side], part_r.at[side], p_send.at[side], p_recv.at[side], 1 - 2 * side))
-        sent[-1].start()
+        joined = total_acc[at, side * cut : (side + 1) * cut] + half_r[side].astype(jnp.float32)
+        part_s[side, 0] = joined.astype(jnp.bfloat16)
+        ship(part_s.at[side, 0], part_r.at[side, 0], p_send.at[side, 0], p_recv.at[side, 0], side)
     down(0, 1)
-    for side in range(2):
-        wait_bytes(part_r.at[side], p_recv.at[side])
+    for kind in (1, 0):
+        for side in range(2):
+            wait_bytes(part_r.at[side, kind], p_recv.at[side, kind])
 
     @pl.loop(0, slots // 16)
     def _(r):
         some = pl.ds(pl.multiple_of(r * 16, 16), 16)
         total = total_acc[some, :] + tok[some, :].astype(jnp.float32) + dbias_ref[...]
-        for side in range(2):
-            total = total + part_r[side, some, :].astype(jnp.float32)
+        low = part_r[0, 0, some, :].astype(jnp.float32) + part_r[1, 1, some, :].astype(jnp.float32)
+        high = part_r[0, 1, some, :].astype(jnp.float32) + part_r[1, 0, some, :].astype(jnp.float32)
+        total = total + jnp.concatenate([low, high], axis=1)
         out_ref[some, :] = norm_rows(total, ogain_ref[...], oshift_ref[...]).astype(jnp.bfloat16)
 
     for copy in sent:
@@ -608,10 +609,10 @@
             pltpu.VMEM((NY * slots, width), f32),
             pltpu.VMEM((2, slots, width // 2), bf16),
             pltpu.VMEM((2, slots, width // 2), bf16),
-            pltpu.VMEM((2, slots, width), bf16),
-            pltpu.VMEM((2, slots, width), bf16),
+            pltpu.VMEM((2, 2, slots, width // 2), bf16),
+            pltpu.VMEM((2, 2, slots, width // 2), bf16),
             dma, dma((DEV,)), dma, dma, dma, dma, dma, dma, dma((4,)), dma((7,)),
-            dma((2,)), dma((2, 5, 4)), dma((2, 4)), dma((4,)), dma((4,)), dma((2,)), dma((2,)), dma((2,)), dma((2,)),
+            dma((2,)), dma((4, 5, 4)), dma((2,)), dma((4,)), dma((4,)), dma((2,)), dma((2,)), dma((2, 2)), dma((2, 2)),
         ],
         compiler_params=pltpu.CompilerParams(collective_id=0, has_side_effects=True, vmem_limit_bytes=LIMIT),
         name="layer",

time: 144 us -> 132 us (0.917)
  Pallas kernels: 142 us -> 129 us
    pallas_call x1, Pallas kernels: 142 us -> 129 us  [on_device(): pl.pallas_call(layer_kernel, out_shape=jax.ShapeDtypeStruct((slots, width...]
where the time goes in v3:
time: 132 us; the launch traced here: 131 us
  Pallas kernels  129 us (98%)
  local copies, waits for them, and re-layouts  1.88 us (1%)
    pallas_call x1, Pallas kernels, on_device(): pl.pallas_call(layer_kernel, out_shape=jax.ShapeDtypeStruct((slots, width...  129 us

profile of v3, /device:TPU:1, one launch (start us, length us, event | category | flops | bytes accessed | tf_op | source)
XLA Modules:
  0.0 131.2 jit_solution(4864418436617564701)
XLA Ops:
  0.0 129.3 %layer.1 = bf16[128,2048]{1,0:T(8,128)(2,1)} custom-call(s32[1,8]{1,0:T(1,128)} %len_ref.1, s32[1,8]{1,0:T(1,128)} %grp_ref.1, bf16[128,2048]{1,0:T(8,128)(2,1)} %q_ref.1, bf16[1,64]{1,0:T(2,128)(2,1)} %bitcast.17, bf16[128,2048]{1,0:T(8,128)(2,1)} %k_in.1, bf16[128,2048]{1,0:T(8,128)(2,1)} %v_in.1, bf16[128,2048]{1,0:T(8,128)(2,1)} %x_in.1, ...), custom_call_target="tpu_custom_call" | custom-call | tf_op jit(solution)/shard_map/layer/pallas_call | solution.py:579
  129.3 1.9 %copy.18 = bf16[128,2048]{1,0:T(8,128)(2,1)} copy(bf16[128,2048]{1,0:T(8,128)(2,1)} %layer.1) | data formatting | bytes 1048576

commit v4 on v3

--- a/solution.py
+++ b/solution.py
@@ -382,14 +382,11 @@
     stage_pairs(2, 4)
     first_direct(0)
     second_own(0, 1)
-    second_own(0, 2)
     stage_pairs(4, 6)
     second_direct(0, 0)
     first_half(0)
-    second_own(0, 3)
+    second_own(0, 2)
     stage_pairs(6, 8)
-    second_direct(0, 1)
-    second_direct(0, 2)
     stage(DEV, 0, False, True, True)
     send_back(DEV - 2)
     stage(DEV + 1, 1, False, False, True)
@@ -400,13 +397,12 @@
     for e in range(NC * DEV // 2):
         bias_all[:, e * HD : (e + 1) * HD] = bias_r[2 * e] + bias_r[2 * e + 1]
 
+    second_direct(0, 1)
+    second_direct(0, 2)
+    second_own(0, 3)
     first_own(1)
     second_own(1, 0)
     second_half(0, 0)
-    second_direct(0, 3)
-    first_direct(1)
-    second_own(1, 1)
-    second_own(1, 2)
     own_answer.wait()
     own_lse.wait()
     wait_bytes(ans_r.at[pl.ds(0, GRP * DEV - 1)], a_recv)
@@ -432,6 +428,10 @@
         below = far_weight + own_weight * own_sum[h]
         mixed[:, cols] = (far_weight * far + own_weight * mixed[:, cols]) / below
 
+    second_direct(0, 3)
+    first_direct(1)
+    second_own(1, 1)
+    second_own(1, 2)
     loads[4].wait()
 
     @pl.loop(0, slots // 16)
@@ -451,12 +451,10 @@
             pl.ds(pos * slots + part * (slots // 2), slots // 2)
         ]
 
-    sent = [
-        y_copy(token(0), token(2), t_send.at[0], t_recv.at[0], 1),
-        y_copy(token(0), token(1), t_send.at[1], t_recv.at[1], -1),
-    ]
-    sent[0].start()
-    sent[1].start()
+    sent = []
+    for n, (part, target, step) in enumerate(((0, 2, 1), (1, 1, -1), (1, 2, 1), (0, 1, -1))):
+        sent.append(y_copy(token(0, part), token(target, part), t_send.at[n], t_recv.at[n], step))
+        sent[-1].start()
     own_weights[0].wait()
     own_weights[1].wait()
     width = q_ref.shape[1]
@@ -476,10 +474,10 @@
             u = u + bias_all[:, cols]
             hidden[rows_, cols] = jax.nn.gelu(u, approximate=True).astype(jnp.bfloat16)
 
-    def down(first, count):
+    def down(first, count, low, high):
         rows_ = pl.ds(first * slots, count * slots)
 
-        @pl.loop(0, width // tile)
+        @pl.loop(low * (width // tile // 2), high * (width // tile // 2))
         def _(n):
             cols = pl.ds(pl.multiple_of(n * tile, tile), tile)
             total_acc[rows_, cols] = jnp.dot(
@@ -493,24 +491,23 @@
     for k in (1, 2, 3):
         second_half(0, k)
     cross_wait(0)
+    for n, (part, origin, step) in enumerate(((0, 2, 1), (1, 1, -1))):
+        wait_bytes(token(origin, part), t_recv.at[n])
+        sent.append(y_copy(token(origin, part), token(3, part), t_send.at[4 + n], t_recv.at[4 + n], step))
+        sent[-1].start()
     second_direct(1, 1)
     second_direct(1, 2)
     up(0, 1)
-    wait_bytes(token(2), t_recv.at[0])
-    wait_bytes(token(1), t_recv.at[1])
-    sent.append(y_copy(token(2, 0), token(3, 0), t_send.at[2], t_recv.at[2], 1))
-    sent.append(y_copy(token(1, 1), token(3, 1), t_send.at[3], t_recv.at[3], -1))
-    sent[2].start()
-    sent[3].start()
+    wait_bytes(token(2, 1), t_recv.at[2])
+    wait_bytes(token(1, 0), t_recv.at[3])
     second_direct(1, 3)
     up(1, 2)
-    wait_bytes(token(3, 0), t_recv.at[2])
-    wait_bytes(token(3, 1), t_recv.at[3])
+    wait_bytes(token(3, 0), t_recv.at[4])
+    wait_bytes(token(3, 1), t_recv.at[5])
     up(3, 1)
     for k in range(4):
         second_half(1, k)
     cross_wait(1)
-    down(3, 1)
     cut = width // 2
 
     def ship(src, dst, send_sem, recv_sem, side):
@@ -518,12 +515,13 @@
         sent[-1].start()
 
     for side in range(2):
+        down(3, 1, side, side + 1)
         half_s[side] = total_acc[3 * slots :, side * cut : (side + 1) * cut].astype(jnp.bfloat16)
         ship(half_s.at[side], half_r.at[side], h_send.at[side], h_recv.at[side], side)
-    down(1, 2)
-    for side in range(2):
+    for rest in range(2):
+        side = 1 - rest
         at = slice((1 + side) * slots, (2 + side) * slots)
-        rest = 1 - side
+        down(1, 2, rest, rest + 1)
         part_s[side, 1] = total_acc[at, rest * cut : (rest + 1) * cut].astype(jnp.bfloat16)
         ship(part_s.at[side, 1], part_r.at[side, 1], p_send.at[side, 1], p_recv.at[side, 1], side)
     for side in range(2):
@@ -532,7 +530,7 @@
         joined = total_acc[at, side * cut : (side + 1) * cut] + half_r[side].astype(jnp.float32)
         part_s[side, 0] = joined.astype(jnp.bfloat16)
         ship(part_s.at[side, 0], part_r.at[side, 0], p_send.at[side, 0], p_recv.at[side, 0], side)
-    down(0, 1)
+    down(0, 1, 0, 2)
     for kind in (1, 0):
         for side in range(2):
             wait_bytes(part_r.at[side, kind], p_recv.at[side, kind])
@@ -612,7 +610,7 @@
             pltpu.VMEM((2, 2, slots, width // 2), bf16),
             pltpu.VMEM((2, 2, slots, width // 2), bf16),
             dma, dma((DEV,)), dma, dma, dma, dma, dma, dma, dma((4,)), dma((7,)),
-            dma((2,)), dma((4, 5, 4)), dma((2,)), dma((4,)), dma((4,)), dma((2,)), dma((2,)), dma((2, 2)), dma((2, 2)),
+            dma((2,)), dma((4, 5, 4)), dma((2,)), dma((6,)), dma((6,)), dma((2,)), dma((2,)), dma((2, 2)), dma((2, 2)),
         ],
         compiler_params=pltpu.CompilerParams(collective_id=0, has_side_effects=True, vmem_limit_bytes=LIMIT),
         name="layer",

time: 132 us -> 126 us (0.955)
  Pallas kernels: 129 us -> 124 us
    pallas_call x1, Pallas kernels: 129 us -> 124 us  [on_device(): pl.pallas_call(layer_kernel, out_shape=jax.ShapeDtypeStruct((slots, width...]
where the time goes in v4:
time: 126 us
  Pallas kernels  124 us (98%)
  local copies, waits for them, and re-layouts  1.88 us (1%)
    pallas_call x1, Pallas kernels, on_device(): pl.pallas_call(layer_kernel, out_shape=jax.ShapeDtypeStruct((slots, width...  124 us

profile of v4, /device:TPU:1, one launch (start us, length us, event | category | flops | bytes accessed | tf_op | source)
XLA Modules:
  0.0 125.6 jit_solution(6478654323061521346)
XLA Ops:
  0.0 123.8 %layer.1 = bf16[128,2048]{1,0:T(8,128)(2,1)} custom-call(s32[1,8]{1,0:T(1,128)} %len_ref.1, s32[1,8]{1,0:T(1,128)} %grp_ref.1, bf16[128,2048]{1,0:T(8,128)(2,1)} %q_ref.1, bf16[1,64]{1,0:T(2,128)(2,1)} %bitcast.17, bf16[128,2048]{1,0:T(8,128)(2,1)} %k_in.1, bf16[128,2048]{1,0:T(8,128)(2,1)} %v_in.1, bf16[128,2048]{1,0:T(8,128)(2,1)} %x_in.1, ...), custom_call_target="tpu_custom_call" | custom-call | tf_op jit(solution)/shard_map/layer/pallas_call | solution.py:577
  123.8 1.9 %copy.18 = bf16[128,2048]{1,0:T(8,128)(2,1)} copy(bf16[128,2048]{1,0:T(8,128)(2,1)} %layer.1) | data formatting | bytes 1048576

commit v5 on v4

--- a/solution.py
+++ b/solution.py
@@ -385,7 +385,6 @@
     stage_pairs(4, 6)
     second_direct(0, 0)
     first_half(0)
-    second_own(0, 2)
     stage_pairs(6, 8)
     stage(DEV, 0, False, True, True)
     send_back(DEV - 2)
@@ -398,7 +397,7 @@
         bias_all[:, e * HD : (e + 1) * HD] = bias_r[2 * e] + bias_r[2 * e + 1]
 
     second_direct(0, 1)
-    second_direct(0, 2)
+    second_own(0, 2)
     second_own(0, 3)
     first_own(1)
     second_own(1, 0)
@@ -428,6 +427,7 @@
         below = far_weight + own_weight * own_sum[h]
         mixed[:, cols] = (far_weight * far + own_weight * mixed[:, cols]) / below
 
+    second_direct(0, 2)
     second_direct(0, 3)
     first_direct(1)
     second_own(1, 1)

time: 126 us -> 128 us (1.016)
  Pallas kernels: 124 us -> 126 us
    pallas_call x1, Pallas kernels: 124 us -> 126 us  [on_device(): pl.pallas_call(layer_kernel, out_shape=jax.ShapeDtypeStruct((slots, width...]
where the time goes in v5:
time: 128 us
  Pallas kernels  126 us (98%)
  local copies, waits for them, and re-layouts  1.88 us (1%)
    pallas_call x1, Pallas kernels, on_device(): pl.pallas_call(layer_kernel, out_shape=jax.ShapeDtypeStruct((slots, width...  126 us

profile of v5, /device:TPU:1, one launch (start us, length us, event | category | flops | bytes accessed | tf_op | source)
XLA Modules:
  0.0 127.5 jit_solution(14738073704558598794)
XLA Ops:
  0.0 125.6 %layer.1 = bf16[128,2048]{1,0:T(8,128)(2,1)} custom-call(s32[1,8]{1,0:T(1,128)} %len_ref.1, s32[1,8]{1,0:T(1,128)} %grp_ref.1, bf16[128,2048]{1,0:T(8,128)(2,1)} %q_ref.1, bf16[1,64]{1,0:T(2,128)(2,1)} %bitcast.17, bf16[128,2048]{1,0:T(8,128)(2,1)} %k_in.1, bf16[128,2048]{1,0:T(8,128)(2,1)} %v_in.1, bf16[128,2048]{1,0:T(8,128)(2,1)} %x_in.1, ...), custom_call_target="tpu_custom_call" | custom-call | tf_op jit(solution)/shard_map/layer/pallas_call | solution.py:577
  125.6 1.9 %copy.18 = bf16[128,2048]{1,0:T(8,128)(2,1)} copy(bf16[128,2048]{1,0:T(8,128)(2,1)} %layer.1) | data formatting | bytes 1048576

commit v6 on v4

--- a/solution.py
+++ b/solution.py
@@ -379,14 +379,14 @@
             stage(2 * pair + 1, 1, True, True, True)
             send_back(2 * pair - 1)
 
-    stage_pairs(2, 4)
+    stage_pairs(2, 3)
     first_direct(0)
     second_own(0, 1)
-    stage_pairs(4, 6)
+    stage_pairs(3, 5)
     second_direct(0, 0)
     first_half(0)
     second_own(0, 2)
-    stage_pairs(6, 8)
+    stage_pairs(5, 8)
     stage(DEV, 0, False, True, True)
     send_back(DEV - 2)
     stage(DEV + 1, 1, False, False, True)

time: 126 us -> 126 us (level)
  no operation moved by 1% of the time
where the time goes in v6:
time: 126 us
  Pallas kernels  124 us (98%)
  local copies, waits for them, and re-layouts  1.88 us (1%)
    pallas_call x1, Pallas kernels, on_device(): pl.pallas_call(layer_kernel, out_shape=jax.ShapeDtypeStruct((slots, width...  124 us

profile of v6, /device:TPU:1, one launch (start us, length us, event | category | flops | bytes accessed | tf_op | source)
XLA Modules:
  0.0 125.7 jit_solution(11475526047824480679)
XLA Ops:
  0.0 123.8 %layer.1 = bf16[128,2048]{1,0:T(8,128)(2,1)} custom-call(s32[1,8]{1,0:T(1,128)} %len_ref.1, s32[1,8]{1,0:T(1,128)} %grp_ref.1, bf16[128,2048]{1,0:T(8,128)(2,1)} %q_ref.1, bf16[1,64]{1,0:T(2,128)(2,1)} %bitcast.17, bf16[128,2048]{1,0:T(8,128)(2,1)} %k_in.1, bf16[128,2048]{1,0:T(8,128)(2,1)} %v_in.1, bf16[128,2048]{1,0:T(8,128)(2,1)} %x_in.1, ...), custom_call_target="tpu_custom_call" | custom-call | tf_op jit(solution)/shard_map/layer/pallas_call | solution.py:577
  123.8 1.9 %copy.18 = bf16[128,2048]{1,0:T(8,128)(2,1)} copy(bf16[128,2048]{1,0:T(8,128)(2,1)} %layer.1) | data formatting | bytes 1048576
